TPU v7x, 32 devices: a whole 2x2x4 slice. The times are simulated.
32 devices in a mesh: row: 4 (over y, x), col: 8 (over z, core).
Axes of the slice: x: 2, y: 2, z: 4, core: 2. Of those that a mesh axis runs over, the one named last changes fastest.
Arguments:
- positions: float32 [2048, 3, 128], P(('row', 'col')), as said below
- velocities: float32 [2048, 3, 128], P(('row', 'col')), may hold values from -4 to 4
- forces: float32 [2048, 3, 128], P(('row', 'col')), may hold values from -60 to 60
- tiles: int32 [4, 8, 1024, 2], P('row', 'col'), may hold values from 0 to 511, as said below
- counts: int32 [4, 8], P('row', 'col'), may hold values from 1 to 1024, as said below
Outputs:
- moved_positions: float32 [2048, 3, 128], P(('row', 'col'))
- new_velocities: float32 [2048, 3, 128], P(('row', 'col'))
- new_forces: float32 [2048, 3, 128], P(('row', 'col'))
Inputs may be any that keep to these rules, and one draw needn't show every extreme that they name: `tiles`: every slot of the list of device (r, c), used or not, holds a pair (li, lj) whose cells are neighbours or equal: li // 64 is c - 1, c or c + 1 modulo 8, lj // 64 is r - 1, r or r + 1 modulo 4, and li % 64 and lj % 64 differ by at most one modulo 64. The slots of one list hold distinct pairs. Entries li lie below 512, entries lj below 256. `counts`: one device's count is exactly 1024. `positions`: each coordinate lies within 0.16 of the matching coordinate of a point of a lattice of spacing 1.2 inside each cell, 4 x 4 x 8 points a cell, one atom at each point.
All inputs are finite; a program needn't handle non-finite values.
Results may differ from a plain program's by a relative error of at most 0.0003.
Values sent between devices are 32-bit elements; how exact they have to be, the bound alone decides.
No kernel may reach another device: no remote copies, remote signals or barrier semaphores. Data moves between devices by JAX's collectives and lax.ppermute only.
A program may use at most 64 MiB of HBM per device.

v0:
```python
import functools

import jax
import jax.numpy as jnp
from jax import lax
from jax.experimental import pallas as pl
from jax.experimental.pallas import tpu as pltpu
from jax.sharding import PartitionSpec as P


TIME_STEP = 0.01
CUT_SQ = 6.25
SHIFT_FORCE = 24.0 * (2.0 * 2.5 ** (-13) - 2.5 ** (-7))
SPACING = 1.2
CELL_XY = 4.8
CELL_Z = 9.6
CELLS = 64
ATOMS = 128
F32 = jnp.float32
VMEM = pl.BlockSpec(memory_space=pltpu.VMEM)
SMEM = pl.BlockSpec(memory_space=pltpu.SMEM)


def lanes():
    return lax.broadcasted_iota(jnp.int32, (8, ATOMS), 1)


def rows8():
    return lax.broadcasted_iota(jnp.int32, (8, ATOMS), 0)


def low_half():
    return lanes() < CELLS


def swap_halves(v):
    return pltpu.roll(v, CELLS, 1)


def from_cell_below(v):
    at_edge = (lanes() & (CELLS - 1)) == 0
    return jnp.where(at_edge, pltpu.roll(v, CELLS + 1, 1), pltpu.roll(v, 1, 1))


def from_cell_above(v):
    at_edge = (lanes() & (CELLS - 1)) == CELLS - 1
    return jnp.where(at_edge, pltpu.roll(v, CELLS - 1, 1), pltpu.roll(v, ATOMS - 1, 1))


def lookup(values, index):
    return jnp.take_along_axis(values, index, axis=1)


def wrapped(step, count):
    step = jnp.where(step < 0, step + count, step)
    return jnp.where(step >= count, step - count, step)


def prepare_kernel(row_count, col_count, pos, vel, frc, tiles, counts,
                   moved_out, half_out, code_out, own_out, mask_out, pay_a, pay_b):
    my_row = lax.axis_index("row")
    my_col = lax.axis_index("col")

    half = vel[...] + (0.5 * TIME_STEP) * frc[...]
    moved = pos[...] + TIME_STEP * half
    half_out[...] = half
    moved_out[...] = moved

    place = pos[...]
    lowest = jnp.min(place, axis=2, keepdims=True)
    site = ((place - lowest) * (1.0 / SPACING) + 0.5).astype(jnp.int32)
    code = (site[1] >> 1) * 64 + site[0] * 16 + (site[1] & 1) * 8 + site[2]
    code_out[...] = code

    point = lax.broadcasted_iota(jnp.int32, (ATOMS, ATOMS), 0)
    spot = lax.broadcasted_iota(jnp.int32, (8, 8 * ATOMS), 1)
    line = lax.broadcasted_iota(jnp.int32, (8, 8 * ATOMS), 0)
    numbers = jnp.where(spot // ATOMS == line, spot % ATOMS, 0).astype(F32).astype(jnp.bfloat16)
    sorted_rows = [[], [], []]
    for group in range(CELLS // 8):
        hot = []
        for b in range(8):
            row = code[group * 8 + b : group * 8 + b + 1, :]
            hot.append(jnp.where(point == row, 1.0, 0.0).astype(jnp.bfloat16))
        hot = jnp.concatenate(hot, axis=1)
        atom = lax.dot_general(numbers, hot, (((1,), (1,)), ((), ())), preferred_element_type=F32)
        atom = atom.astype(jnp.int32)
        for k in range(3):
            sorted_rows[k].append(lookup(moved[k, group * 8 : group * 8 + 8, :], atom))

    own = []
    for k in range(3):
        cells_first = jnp.concatenate(sorted_rows[k], axis=0)
        both = jnp.concatenate([cells_first, pltpu.roll(cells_first, CELLS, 1)], axis=0)
        own.append(jnp.swapaxes(both, 0, 1)[:CELLS].reshape(4, 2, 8, ATOMS))
        own_out[k] = own[k]

    left = tiles[0:1, :]
    right = tiles[1:2, :]
    used = counts[0, 0]
    dx = 2 - wrapped(my_row - (right >> 6) + 1, row_count)
    dy = 2 - wrapped((left >> 6) - my_col + 1, col_count)
    dz = 2 - (((left & 63) - (right & 63) + 1) & 63)
    alive = lax.broadcasted_iota(jnp.int32, left.shape, 1) < used
    kind = jnp.where(alive, dy * 16 + dz * 3 + dx, -1)
    slots = left.shape[1]
    kind_hot = lax.broadcasted_iota(jnp.int32, (48, slots), 0) == kind
    cell_hot = (lax.broadcasted_iota(jnp.int32, (ATOMS, slots), 0) & 63) == (right & 63)
    mask = lax.dot_general(
        jnp.where(kind_hot, 1.0, 0.0).astype(jnp.bfloat16),
        jnp.where(cell_hot, 1.0, 0.0).astype(jnp.bfloat16),
        (((1,), (1,)), ((), ())), preferred_element_type=F32,
    ).reshape(3, 2, 8, ATOMS)
    mask_out[...] = mask[1]

    def pack(to_upper, to_lower):
        lo = low_half()
        for k in range(3):
            for x in range(4):
                first, second = own[k][x, 0], own[k][x, 1]
                up = jnp.where(lo, swap_halves(first), second)
                down = jnp.where(lo, first, swap_halves(second))
                if k == 1:
                    up = up - CELL_XY
                    down = down + CELL_XY
                to_upper[k * 4 + x] = up
                to_lower[k * 4 + x] = down
        to_upper[12:14] = mask[0]
        to_lower[12:14] = mask[2]

    odd = (my_col & 1) == 1

    @pl.when(odd)
    def _():
        pack(pay_a, pay_b)

    @pl.when(jnp.logical_not(odd))
    def _():
        pack(pay_b, pay_a)


def row_frames(own, frames):
    for k in range(3):
        for x in range(4):
            for yy in range(2):
                v = own[k, x, yy]
                below = from_cell_below(v)
                above = from_cell_above(v)
                if k == 2:
                    below = below - CELL_Z
                    above = above + CELL_Z
                for kz in (-2, -1, 0, 1, 2):
                    if kz == 0:
                        out = v
                    elif kz > 0:
                        out = pltpu.roll(jnp.where(rows8() >= 8 - kz, below, v), kz, 0)
                    else:
                        out = pltpu.roll(jnp.where(rows8() < -kz, above, v), 8 + kz, 0)
                    frames[kz + 2, k, x, yy] = out


def limits(mask_low, mask_own, mask_high, kz, dx, group):
    def row(mask, dz):
        index = (dz + 1) * 3 + dx + 1
        return jnp.broadcast_to(mask[index // 8, index % 8 : index % 8 + 1, :], (8, ATOMS))

    def both(dz):
        if group == 0:
            return jnp.where(low_half(), row(mask_low, dz), row(mask_own, dz))
        if group == 2:
            return jnp.where(low_half(), row(mask_own, dz), row(mask_high, dz))
        return row(mask_own, dz)

    inner = both(0)
    if kz > 0:
        inner = jnp.where(rows8() < kz, both(1), inner)
    if kz < 0:
        inner = jnp.where(rows8() >= 8 + kz, both(-1), inner)
    return inner * CUT_SQ


def spread(first, second, lower, upper):
    lo = low_half()
    return [
        jnp.where(lo, lower, swap_halves(first)),
        swap_halves(jnp.where(lo, second, lower)),
        first,
        second,
        swap_halves(jnp.where(lo, upper, first)),
        jnp.where(lo, swap_halves(second), upper),
    ]


def add_pairs(frames, before, total, partner, limit, columns, rows):
    for kz in (-2, -1, 0, 1, 2):
        for x in range(4):
            for yy in range(2):
                mine = [frames[kz + 2, k, x, yy] for k in range(3)]
                acc = [None if before is None else before[kz + 2, k, x, yy] for k in range(3)]
                for kx in (-2, -1, 0, 1, 2):
                    for ky in (-2, -1, 0, 1, 2):
                        if (abs(kx) == 2) + (abs(ky) == 2) + (abs(kz) == 2) > 1:
                            continue
                        if kx == 0 and ky == 0 and kz == 0:
                            continue
                        if x + kx not in columns or yy + ky + 2 not in rows:
                            continue
                        m = yy + ky + 2
                        away = [mine[k] - partner(k, x + kx, m) for k in range(3)]
                        dist = away[0] * away[0] + away[1] * away[1] + away[2] * away[2]
                        inside = (dist < limit(kz, (x + kx) // 4, m // 2)) & (dist > 0.25)
                        inv = lax.rsqrt(dist)
                        inv_sq = inv * inv
                        inv_six = inv_sq * inv_sq * inv_sq
                        weight = inv_sq * (inv_six * (48.0 * inv_six - 24.0)) - SHIFT_FORCE * inv
                        weight = jnp.where(inside, weight, 0.0)
                        for k in range(3):
                            term = weight * away[k]
                            acc[k] = term if acc[k] is None else acc[k] + term
                for k in range(3):
                    total[kz + 2, k, x, yy] = jnp.zeros((8, ATOMS), F32) if acc[k] is None else acc[k]


def own_kernel(own, mask, frames, total):
    row_frames(own, frames)
    table = {kz: limits(None, mask, None, kz, 0, 1) for kz in (-2, -1, 0, 1, 2)}
    add_pairs(frames, None, total, lambda k, x, m: own[k, x, m - 2], lambda kz, dx, g: table[kz],
              (0, 1, 2, 3), (2, 3))


def relay_kernel(own, got_a, got_b, pay_a, pay_b):
    col_odd = (lax.axis_index("col") & 1) == 1
    row_odd = (lax.axis_index("row") & 1) == 1

    def pack(ref, columns, offset):
        for k in range(3):
            for n, x in enumerate(columns):
                from_a, from_b = got_a[k * 4 + x], got_b[k * 4 + x]
                parts = [own[k, x, 0], own[k, x, 1],
                         jnp.where(col_odd, from_b, from_a), jnp.where(col_odd, from_a, from_b)]
                for i in range(4):
                    ref[k, n, i] = parts[i] + offset if k == 0 else parts[i]

    @pl.when(row_odd)
    def _():
        pack(pay_a, (2, 3), -CELL_XY)
        pack(pay_b, (0, 1), CELL_XY)

    @pl.when(jnp.logical_not(row_odd))
    def _():
        pack(pay_b, (2, 3), -CELL_XY)
        pack(pay_a, (0, 1), CELL_XY)


def column_kernel(own, mask, got_a, got_b, frames, total_in, total, table, near, outer):
    col_odd = (lax.axis_index("col") & 1) == 1
    for k in range(3):
        for x in range(4):
            from_a, from_b = got_a[k * 4 + x], got_b[k * 4 + x]
            lower = jnp.where(col_odd, from_b, from_a)
            upper = jnp.where(col_odd, from_a, from_b)
            six = spread(own[k, x, 0], own[k, x, 1], lower, upper)
            near[k, x, 0] = six[0]
            near[k, x, 1] = six[1]
            near[k, x, 2] = six[4]
            near[k, x, 3] = six[5]
    mask_a, mask_b = got_a[12:14], got_b[12:14]
    mask_low = jnp.where(col_odd, mask_b, mask_a)
    mask_high = jnp.where(col_odd, mask_a, mask_b)
    mask_own = mask[...]
    for kz in (-2, -1, 0, 1, 2):
        for g in range(3):
            for n, dx in enumerate((-1, 1)):
                table[kz + 2, n, g] = limits(mask_low, mask_own, mask_high, kz, dx, g)
            if g != 1:
                outer[kz + 2, g // 2] = limits(mask_low, mask_own, mask_high, kz, 0, g)
    add_pairs(frames, total_in, total, lambda k, x, m: near[k, x, m if m < 2 else m - 2],
              lambda kz, dx, g: outer[kz + 2, g // 2], (0, 1, 2, 3), (0, 1, 4, 5))


def finish_kernel(got_a, got_b, frames, total_in, table, half, code, new_vel, new_frc, total, side):
    row_odd = (lax.axis_index("row") & 1) == 1
    for k in range(3):
        for n in range(2):
            for s in range(2):
                parts = [jnp.where(row_odd == (s == 0), got_b[k, n, i], got_a[k, n, i]) for i in range(4)]
                six = spread(*parts)
                for m in range(6):
                    side[s, k, n, m] = six[m]

    def partner(k, x, m):
        return side[0, k, x + 2, m] if x < 0 else side[1, k, x - 4, m]

    add_pairs(frames, total_in, total, partner, lambda kz, dx, g: table[kz + 2, 0 if dx < 0 else 1, g],
              (-2, -1, 4, 5), (0, 1, 2, 3, 4, 5))

    row = rows8()
    lo = low_half()[0:1]
    for k in range(3):
        stacked = []
        for x in range(4):
            for yy in range(2):
                one_up = pltpu.roll(total[3, k, x, yy], 7, 0)
                two_up = pltpu.roll(total[4, k, x, yy], 6, 0)
                one_down = pltpu.roll(total[1, k, x, yy], 1, 0)
                two_down = pltpu.roll(total[0, k, x, yy], 2, 0)
                inner = total[2, k, x, yy] + jnp.where(row < 7, one_up, 0.0) + jnp.where(row < 6, two_up, 0.0)
                inner = inner + jnp.where(row > 0, one_down, 0.0) + jnp.where(row > 1, two_down, 0.0)
                above = jnp.where(row < 7, 0.0, one_up) + jnp.where(row < 6, 0.0, two_up)
                below = jnp.where(row > 0, 0.0, one_down) + jnp.where(row > 1, 0.0, two_down)
                stacked.append(inner + from_cell_above(above) + from_cell_below(below))
        lattice = jnp.concatenate(stacked, axis=0)
        flipped = jnp.swapaxes(jnp.concatenate([lattice, lattice], axis=0), 0, 1)
        cells_first = jnp.where(lo, flipped[:CELLS], flipped[CELLS:])
        for g in range(8):
            rows = slice(g * 8, g * 8 + 8)
            value = lookup(cells_first[rows], code[rows, :])
            new_frc[k, rows, :] = value
            new_vel[k, rows, :] = half[k, rows, :] + (0.5 * TIME_STEP) * value


def kernel_call(body, outs, args, specs=None, scratch=(), flops=0, name=None):
    moved = sum(4 * a.size for a in args) + sum(4 * s.size for s in outs)
    return pl.pallas_call(
        body,
        out_shape=outs,
        in_specs=[VMEM] * len(args) if specs is None else specs,
        out_specs=[VMEM] * len(outs),
        scratch_shapes=list(scratch),
        compiler_params=pltpu.CompilerParams(vmem_limit_bytes=8 << 20),
        cost_estimate=pl.CostEstimate(flops=flops, bytes_accessed=moved, transcendentals=0),
        name=name,
    )(*args)


def pairing(count, odd):
    if odd:
        return [(i, (i + 1) % count if i % 2 else (i - 1) % count) for i in range(count)]
    return [(i, i ^ 1) for i in range(count)]


def exchange(first, second, axis):
    count = lax.axis_size(axis)
    return (lax.ppermute(first, axis, pairing(count, True)), lax.ppermute(second, axis, pairing(count, False)))


def per_device(positions, velocities, forces, tiles, counts):
    blocks, _, atoms = positions.shape
    assert blocks == CELLS and atoms == ATOMS
    row_count, col_count = lax.axis_size("row"), lax.axis_size("col")
    assert row_count % 2 == 0 and col_count % 2 == 0 and min(row_count, col_count) > 2
    by_component = [jnp.transpose(a, (1, 0, 2)) for a in (positions, velocities, forces)]
    tile_rows = jnp.transpose(tiles[0, 0], (1, 0))

    def f32(*shape):
        return jax.ShapeDtypeStruct(shape, F32)

    span = f32(3, CELLS, ATOMS)
    lattice = f32(3, 4, 2, 8, ATOMS)
    moved, half, code, own, mask, pay_a, pay_b = kernel_call(
        functools.partial(prepare_kernel, row_count, col_count),
        [span, span, jax.ShapeDtypeStruct((CELLS, ATOMS), jnp.int32), lattice, f32(2, 8, ATOMS),
         f32(14, 8, ATOMS), f32(14, 8, ATOMS)],
        [*by_component, tile_rows, counts],
        specs=[VMEM, VMEM, VMEM, VMEM, SMEM], name="prepare",
    )
    got_a, got_b = exchange(pay_a, pay_b, "col")
    frames, total = kernel_call(own_kernel, [f32(5, 3, 4, 2, 8, ATOMS)] * 2, [own, mask], flops=10**8, name="own")
    side_a, side_b = kernel_call(relay_kernel, [f32(3, 2, 4, 8, ATOMS)] * 2, [own, got_a, got_b], name="relay")
    far_a, far_b = exchange(side_a, side_b, "row")
    total, table = kernel_call(
        column_kernel, [f32(5, 3, 4, 2, 8, ATOMS), f32(5, 2, 3, 8, ATOMS)],
        [own, mask, got_a, got_b, frames, total], flops=10**8, name="column",
        scratch=[pltpu.VMEM((3, 4, 4, 8, ATOMS), F32), pltpu.VMEM((5, 2, 8, ATOMS), F32)],
    )
    new_vel, new_frc = kernel_call(
        finish_kernel, [span, span], [far_a, far_b, frames, total, table, half, code], flops=10**8, name="finish",
        scratch=[pltpu.VMEM((5, 3, 4, 2, 8, ATOMS), F32), pltpu.VMEM((2, 3, 2, 6, 8, ATOMS), F32)],
    )
    return tuple(jnp.transpose(a, (1, 0, 2)) for a in (moved, new_vel, new_frc))


def solution(mesh):
    in_specs = (
        P(("row", "col"), None, None),
        P(("row", "col"), None, None),
        P(("row", "col"), None, None),
        P("row", "col", None, None),
        P("row", "col"),
    )
    out_specs = (
        P(("row", "col"), None, None),
        P(("row", "col"), None, None),
        P(("row", "col"), None, None),
    )
    return jax.shard_map(
        per_device, mesh=mesh, in_specs=in_specs, out_specs=out_specs, check_vma=False
    )
```

profile of v0, /device:TPU:0, one launch (start us, length us, event | category | flops | bytes accessed | tf_op | source)
XLA Modules:
  0.0 21.7 jit_solution(14702894327039272674)
XLA Ops:
  0.6 0.0 copy-start.3
  1.3 0.0 copy-done.3
  1.3 0.0 copy-start
  1.3 0.9 %copy-done = f32[64,3,128]{2,0,1:T(8,128)S(1)} copy-done((f32[64,3,128]{2,0,1:T(8,128)S(1)}, f32[64,3,128]{2,0,1:T(8,128)}, u32[]{:S(2)}) %copy-start) | copy-done | bytes 98328
  2.2 0.0 copy-start.1
  2.2 0.9 %copy-done.1 = f32[64,3,128]{2,0,1:T(8,128)S(1)} copy-done((f32[64,3,128]{2,0,1:T(8,128)S(1)}, f32[64,3,128]{2,0,1:T(8,128)}, u32[]{:S(2)}) %copy-start.1) | copy-done | bytes 98328
  3.1 0.0 copy-start.2
  3.1 0.9 %copy-done.2 = f32[64,3,128]{2,0,1:T(8,128)S(1)} copy-done((f32[64,3,128]{2,0,1:T(8,128)S(1)}, f32[64,3,128]{2,0,1:T(8,128)}, u32[]{:S(2)}) %copy-start.2) | copy-done | bytes 98328
  4.0 1.8 %prepare.1 = (f32[3,64,128]{2,1,0:T(8,128)}, f32[3,64,128]{2,1,0:T(8,128)S(1)}, s32[64,128]{1,0:T(8,128)S(1)}, f32[3,4,2,8,128]{4,3,2,1,0:T(8,128)S(1)}, f32[2,8...) custom-call(f32[3,64,128]{2,1,0:T(8,128)S(1)} %bitcast.9, f32[3,64,128]{2,1,0:T(8,128)S(1)} %bitcast.10, ...), custom_call_target="tpu_custom_call" | custom-call | bytes 753668 | tf_op jit(solution)/shard_map/prepare/pallas_call | solution.py:324
  5.8 4.5 %collective-permute-start = (f32[14,8,128]{2,1,0:T(8,128)S(1)}, f32[14,8,128]{2,1,0:T(8,128)S(1)}, u32[]{:S(2)}, u32[]{:S(2)}) collective-permute-start(f32[14,8,128]{2,1,0:T(8,128)S(1)} %get-tuple-element.20), channel_id=1, source_target_pairs={{0,7},{1,2},{2,1},{3,4},{4,3},{5,6},{6,5},{7,0},{8,15},{9,10},{10,... | collective-permute-start | bytes 172040 | tf_op jit(solution)/shard_map/ppermute | solution.py:344
  10.3 0.0 collective-permute-start.1
  10.3 2.0 %collective-permute-done.got_a = f32[14,8,128]{2,1,0:T(8,128)S(1)} collective-permute-done((f32[14,8,128]{2,1,0:T(8,128)S(1)}, f32[14,8,128]{2,1,0:T(8,128)S(1)}, u32[]{:S(2)}, u32[]{:S(2)}) %collective-permute-start) | collective-permute-done | bytes 57376 | tf_op jit(solution)/shard_map/ppermute | solution.py:344
  12.2 0.0 collective-permute-done.1.got_b
  12.3 3.2 %collective-permute-start.2 = (f32[3,2,4,8,128]{4,3,2,1,0:T(8,128)S(1)}, f32[3,2,4,8,128]{4,3,2,1,0:T(8,128)S(1)}, u32[]{:S(2)}, u32[]{:S(2)}) collective-permute-start(f32[3,2,4,8,128]{4,3,2,1,0:T(8,128)S(1)} %get-tuple-element.22), channel_id=1, source_target_pairs={{0,24},{8,16},{16,8},{24,0},{1,25},{9,17},{17,9},{25,1},{2,26},{10... | collective-permute-start | bytes 294920 | tf_op jit(solution)/shard_map/ppermute | solution.py:344
  15.5 0.5 %collective-permute-start.3 = (f32[3,2,4,8,128]{4,3,2,1,0:T(8,128)S(1)}, f32[3,2,4,8,128]{4,3,2,1,0:T(8,128)S(1)}, u32[]{:S(2)}, u32[]{:S(2)}) collective-permute-start(f32[3,2,4,8,128]{4,3,2,1,0:T(8,128)S(1)} %get-tuple-element.23), channel_id=1, source_target_pairs={{0,8},{8,0},{16,24},{24,16},{1,9},{9,1},{17,25},{25,17},{2,10},{10... | collective-permute-start | bytes 294920 | tf_op jit(solution)/shard_map/ppermute | solution.py:344
  16.0 1.0 %own.1 = (f32[5,3,4,2,8,128]{5,4,3,2,1,0:T(8,128)S(1)}, f32[5,3,4,2,8,128]{5,4,3,2,1,0:T(8,128)S(1)}) custom-call(f32[3,4,2,8,128]{4,3,2,1,0:T(8,128)S(1)} %get-tuple-element.19.own, f32[2,8,128]{2,1,0:T(8,128)S(1)} %get-tuple-element.24.mask), custom_call_target="tpu_custom_call" | custom-call | flops 100000000 | bytes 1089536 | tf_op jit(solution)/shard_map/own/pallas_call | solution.py:324
  17.0 1.0 %column.1 = (f32[5,3,4,2,8,128]{5,4,3,2,1,0:T(8,128)S(1)}, f32[5,2,3,8,128]{4,3,2,1,0:T(8,128)S(1)}) custom-call(f32[3,4,2,8,128]{4,3,2,1,0:T(8,128)S(1)} %get-tuple-element.19.own, f32[2,8,128]{2,1,0:T(8,128)S(1)} %get-tuple-element.24.mask, f32[14,8,128]{2,1,0:T(8,128)S(1)} %collective-permute-done.got_a, f32[14,8,128]{2,1,0:T(8,128)S(1)} %collective-permute-done.1.got_b, ...), custom_call_target="tpu_custom_call" | custom-call | flops 100000000 | bytes 1818624 | tf_op jit(solution)/shard_map/column/pallas_call | solution.py:324
  18.0 0.5 %collective-permute-done.2.got_a = f32[3,2,4,8,128]{4,3,2,1,0:T(8,128)S(1)} collective-permute-done((f32[3,2,4,8,128]{4,3,2,1,0:T(8,128)S(1)}, f32[3,2,4,8,128]{4,3,2,1,0:T(8,128)S(1)}, u32[]{:S(2)}, u32[]{:S(2)}) %collective-permute-start.2) | collective-permute-done | bytes 98336 | tf_op jit(solution)/shard_map/ppermute | solution.py:344
  18.6 1.5 %collective-permute-done.3.got_b = f32[3,2,4,8,128]{4,3,2,1,0:T(8,128)S(1)} collective-permute-done((f32[3,2,4,8,128]{4,3,2,1,0:T(8,128)S(1)}, f32[3,2,4,8,128]{4,3,2,1,0:T(8,128)S(1)}, u32[]{:S(2)}, u32[]{:S(2)}) %collective-permute-start.3) | collective-permute-done | bytes 98336 | tf_op jit(solution)/shard_map/ppermute | solution.py:344
  20.1 1.7 %finish.1 = (f32[3,64,128]{2,1,0:T(8,128)}, f32[3,64,128]{2,1,0:T(8,128)}) custom-call(f32[3,2,4,8,128]{4,3,2,1,0:T(8,128)S(1)} %collective-permute-done.2.got_a, f32[3,2,4,8,128]{4,3,2,1,0:T(8,128)S(1)} %collective-permute-done.3.got_b, f32[5,3,4,2,8,128]{5,4,3,2,1,0:T(8,128)S(1)} %get-tuple-element.25.frames, ...), custom_call_target="tpu_custom_call" | custom-call | flops 100000000 | bytes 1630208 | tf_op jit(solution)/shard_map/finish/pallas_call | solution.py:324
  (1 shorter events, 0.0 us)
Async XLA Ops:
  0.6 0.7 %copy-start.3 = (s32[1,1,1024,2]{2,3,1,0:T(2,128)S(1)}, s32[1,1,1024,2]{2,3,1,0:T(2,128)}, u32[]{:S(2)}) copy-start(s32[1,1,1024,2]{2,3,1,0:T(2,128)} %param.8) | copy-start | bytes 24580
  1.3 0.9 %copy-start = (f32[64,3,128]{2,0,1:T(8,128)S(1)}, f32[64,3,128]{2,0,1:T(8,128)}, u32[]{:S(2)}) copy-start(f32[64,3,128]{2,0,1:T(8,128)} %param.5) | copy-start | bytes 294916
  2.2 0.9 %copy-start.1 = (f32[64,3,128]{2,0,1:T(8,128)S(1)}, f32[64,3,128]{2,0,1:T(8,128)}, u32[]{:S(2)}) copy-start(f32[64,3,128]{2,0,1:T(8,128)} %param.6) | copy-start | bytes 294916
  3.1 0.9 %copy-start.2 = (f32[64,3,128]{2,0,1:T(8,128)S(1)}, f32[64,3,128]{2,0,1:T(8,128)}, u32[]{:S(2)}) copy-start(f32[64,3,128]{2,0,1:T(8,128)} %param.7) | copy-start | bytes 294916
  5.8 6.5 %collective-permute-start = (f32[14,8,128]{2,1,0:T(8,128)S(1)}, f32[14,8,128]{2,1,0:T(8,128)S(1)}, u32[]{:S(2)}, u32[]{:S(2)}) collective-permute-start(f32[14,8,128]{2,1,0:T(8,128)S(1)} %get-tuple-element.20), channel_id=1, source_target_pairs={{0,7},{1,2},{2,1},{3,4},{4,3},{5,6},{6,5},{7,0},{8,15},{9,10},{10,... | collective-permute-start | bytes 172040 | tf_op jit(solution)/shard_map/ppermute | solution.py:344
  10.3 2.0 %collective-permute-start.1 = (f32[14,8,128]{2,1,0:T(8,128)S(1)}, f32[14,8,128]{2,1,0:T(8,128)S(1)}, u32[]{:S(2)}, u32[]{:S(2)}) collective-permute-start(f32[14,8,128]{2,1,0:T(8,128)S(1)} %get-tuple-element.21), channel_id=1, source_target_pairs={{0,1},{1,0},{2,3},{3,2},{4,5},{5,4},{6,7},{7,6},{8,9},{9,8},{10,11... | collective-permute-start | bytes 172040 | tf_op jit(solution)/shard_map/ppermute | solution.py:344
  12.3 6.3 %collective-permute-start.2 = (f32[3,2,4,8,128]{4,3,2,1,0:T(8,128)S(1)}, f32[3,2,4,8,128]{4,3,2,1,0:T(8,128)S(1)}, u32[]{:S(2)}, u32[]{:S(2)}) collective-permute-start(f32[3,2,4,8,128]{4,3,2,1,0:T(8,128)S(1)} %get-tuple-element.22), channel_id=1, source_target_pairs={{0,24},{8,16},{16,8},{24,0},{1,25},{9,17},{17,9},{25,1},{2,26},{10... | collective-permute-start | bytes 294920 | tf_op jit(solution)/shard_map/ppermute | solution.py:344
  15.5 4.6 %collective-permute-start.3 = (f32[3,2,4,8,128]{4,3,2,1,0:T(8,128)S(1)}, f32[3,2,4,8,128]{4,3,2,1,0:T(8,128)S(1)}, u32[]{:S(2)}, u32[]{:S(2)}) collective-permute-start(f32[3,2,4,8,128]{4,3,2,1,0:T(8,128)S(1)} %get-tuple-element.23), channel_id=1, source_target_pairs={{0,8},{8,0},{16,24},{24,16},{1,9},{9,1},{17,25},{25,17},{2,10},{10... | collective-permute-start | bytes 294920 | tf_op jit(solution)/shard_map/ppermute | solution.py:344
where the time goes:
time: 22 us; the launch traced here: 21.7 us
  starting transfers between devices  8.22 us (37%)
  Pallas kernels  5.5 us (25%)
  waiting for transfers between devices  4 us (18%)
  local copies, waits for them, and re-layouts  2.71 us (12%)
  between operations  1.32 us (6%)
    ppermute x2, starting transfers between devices, exchange(): lax.ppermute(first, axis, pairing(count, True))  7.69 us
    pallas_call x5, Pallas kernels, kernel_call(): pl.pallas_call(body, out_shape=outs, in_specs=[VMEM] * len(args) if specs...  5.5 us
    unnamed x8, local copies, waits for them, and re-layouts  2.71 us
    ppermute x2, waiting for transfers between devices, exchange(): lax.ppermute(first, axis, pairing(count, True))  2.5 us
    ppermute x2, waiting for transfers between devices, exchange(): lax.ppermute(second, axis, pairing(count, False))  1.5 us
    ppermute x2, starting transfers between devices, exchange(): lax.ppermute(second, axis, pairing(count, False))  0.53 us
  transfers between devices with their start and end apart: 4, of which 3 were waited for; matrix products, arithmetic and copies ran while one was open for 0% of the time, Pallas kernels for 9%

commit v1 on v0

v1 whole, which is shorter than its diff:
```python
import functools

import jax
import jax.numpy as jnp
from jax import lax
from jax.experimental import pallas as pl
from jax.experimental.pallas import tpu as pltpu
from jax.sharding import PartitionSpec as P


TIME_STEP = 0.01
CUT_SQ = 6.25
SHIFT_FORCE = 24.0 * (2.0 * 2.5 ** (-13) - 2.5 ** (-7))
SPACING = 1.2
CELL_XY = 4.8
CELL_Z = 9.6
CELLS = 64
ATOMS = 128
F32 = jnp.float32
VMEM = pl.BlockSpec(memory_space=pltpu.VMEM)
SMEM = pl.BlockSpec(memory_space=pltpu.SMEM)
HBM = pl.BlockSpec(memory_space=pltpu.HBM)


def lanes():
    return lax.broadcasted_iota(jnp.int32, (8, ATOMS), 1)


def rows8():
    return lax.broadcasted_iota(jnp.int32, (8, ATOMS), 0)


def low_half():
    return lanes() < CELLS


def swap_halves(v):
    return pltpu.roll(v, CELLS, 1)


def from_cell_below(v):
    at_edge = (lanes() & (CELLS - 1)) == 0
    return jnp.where(at_edge, pltpu.roll(v, CELLS + 1, 1), pltpu.roll(v, 1, 1))


def from_cell_above(v):
    at_edge = (lanes() & (CELLS - 1)) == CELLS - 1
    return jnp.where(at_edge, pltpu.roll(v, CELLS - 1, 1), pltpu.roll(v, ATOMS - 1, 1))


def lookup(values, index):
    return jnp.take_along_axis(values, index, axis=1)


def wrapped(step, count):
    step = jnp.where(step < 0, step + count, step)
    return jnp.where(step >= count, step - count, step)


def by_parity(index, pack, first, second):
    odd = (index & 1) == 1

    @pl.when(odd)
    def _():
        pack(first, second)

    @pl.when(jnp.logical_not(odd))
    def _():
        pack(second, first)


def prepare_kernel(row_count, col_count, pos_hbm, vel_hbm, frc_hbm, tiles_hbm, counts,
                   moved_out, half_out, code_out, own_out, mask_out, pay_a, pay_b, face_a, face_b,
                   pos, vel, frc, tiles, sems):
    my_row = lax.axis_index("row")
    my_col = lax.axis_index("col")
    copies = [pltpu.make_async_copy(tiles_hbm, tiles, sems.at[9])]
    for i, (source, target) in enumerate([(pos_hbm, pos), (vel_hbm, vel), (frc_hbm, frc)]):
        for k in range(3):
            copies.append(pltpu.make_async_copy(source.at[k], target.at[k], sems.at[i * 3 + k]))
    for copy in copies[1:4] + copies[:1] + copies[4:]:
        copy.start()
    for copy in copies[1:4]:
        copy.wait()

    place = pos[...]
    lowest = jnp.min(place, axis=2, keepdims=True)
    site = ((place - lowest) * (1.0 / SPACING) + 0.5).astype(jnp.int32)
    code = (site[1] >> 1) * 64 + site[0] * 16 + (site[1] & 1) * 8 + site[2]
    code_out[...] = code

    high, low = code >> 4, code & 15
    number = lax.broadcasted_iota(jnp.int32, (8, ATOMS), 1)
    digit = lax.broadcasted_iota(jnp.int32, (16, ATOMS), 0)
    pick = rows8() * 16 + (lanes() & 15)
    order = []
    for g in range(CELLS // 8):
        rows = slice(g * 8, g * 8 + 8)
        left = [jnp.where(high[rows] == h, number, 0).astype(F32) for h in range(8)]
        right = [jnp.where(digit == low[b : b + 1], 1.0, 0.0).astype(F32) for b in range(g * 8, g * 8 + 8)]
        found = lax.dot_general(
            jnp.concatenate(left, axis=0).astype(jnp.bfloat16), jnp.concatenate(right, axis=0).astype(jnp.bfloat16),
            (((1,), (1,)), ((), ())), preferred_element_type=F32,
        ).astype(jnp.int32)
        atom = lookup(found[:8], pick)
        for h in range(1, 8):
            atom = jnp.where(lanes() >= h * 16, lookup(found[h * 8 : h * 8 + 8], pick), atom)
        order.append(atom)

    for copy in copies[:1] + copies[4:]:
        copy.wait()
    half = vel[...] + (0.5 * TIME_STEP) * frc[...]
    moved = pos[...] + TIME_STEP * half
    half_out[...] = half
    moved_out[...] = moved

    own = []
    for k in range(3):
        cells_first = jnp.concatenate(
            [lookup(moved[k, g * 8 : g * 8 + 8, :], order[g]) for g in range(CELLS // 8)], axis=0
        )
        both = jnp.concatenate([cells_first, pltpu.roll(cells_first, CELLS, 1)], axis=0)
        own.append(jnp.swapaxes(both, 0, 1)[:CELLS].reshape(4, 2, 8, ATOMS))
        own_out[k] = own[k]

    left = tiles[0:1, :]
    right = tiles[1:2, :]
    used = counts[0, 0]
    dx = 2 - wrapped(my_row - (right >> 6) + 1, row_count)
    dy = 2 - wrapped((left >> 6) - my_col + 1, col_count)
    dz = 2 - (((left & 63) - (right & 63) + 1) & 63)
    alive = lax.broadcasted_iota(jnp.int32, left.shape, 1) < used
    kind = jnp.where(alive, dy * 16 + dz * 3 + dx, -1)
    slots = left.shape[1]
    kind_hot = lax.broadcasted_iota(jnp.int32, (48, slots), 0) == kind
    cell_hot = (lax.broadcasted_iota(jnp.int32, (ATOMS, slots), 0) & 63) == (right & 63)
    mask = lax.dot_general(
        jnp.where(kind_hot, 1.0, 0.0).astype(jnp.bfloat16),
        jnp.where(cell_hot, 1.0, 0.0).astype(jnp.bfloat16),
        (((1,), (1,)), ((), ())), preferred_element_type=F32,
    ).reshape(3, 2, 8, ATOMS)
    mask_out[...] = mask[1]

    def pack(to_upper, to_lower):
        lo = low_half()
        for k in range(3):
            for x in range(4):
                first, second = own[k][x, 0], own[k][x, 1]
                up = jnp.where(lo, swap_halves(first), second)
                down = jnp.where(lo, first, swap_halves(second))
                if k == 1:
                    up = up - CELL_XY
                    down = down + CELL_XY
                to_upper[k * 4 + x] = up
                to_lower[k * 4 + x] = down
        to_upper[12:14] = mask[0]
        to_lower[12:14] = mask[2]

    def pack_faces(to_upper, to_lower):
        for k in range(3):
            for yy in range(2):
                for n in range(2):
                    up, down = own[k][2 + n, yy], own[k][n, yy]
                    to_upper[k, n, yy] = up - CELL_XY if k == 0 else up
                    to_lower[k, n, yy] = down + CELL_XY if k == 0 else down

    by_parity(my_col, pack, pay_a, pay_b)
    by_parity(my_row, pack_faces, face_a, face_b)


def row_frames(own, frames):
    for k in range(3):
        for x in range(4):
            for yy in range(2):
                v = own[k, x, yy]
                below = from_cell_below(v)
                above = from_cell_above(v)
                if k == 2:
                    below = below - CELL_Z
                    above = above + CELL_Z
                for kz in (-2, -1, 0, 1, 2):
                    if kz == 0:
                        out = v
                    elif kz > 0:
                        out = pltpu.roll(jnp.where(rows8() >= 8 - kz, below, v), kz, 0)
                    else:
                        out = pltpu.roll(jnp.where(rows8() < -kz, above, v), 8 + kz, 0)
                    frames[kz + 2, k, x, yy] = out


def limits(mask_low, mask_own, mask_high, kz, dx, group):
    def row(mask, dz):
        index = (dz + 1) * 3 + dx + 1
        return jnp.broadcast_to(mask[index // 8, index % 8 : index % 8 + 1, :], (8, ATOMS))

    def both(dz):
        if group == 0:
            return jnp.where(low_half(), row(mask_low, dz), row(mask_own, dz))
        if group == 2:
            return jnp.where(low_half(), row(mask_own, dz), row(mask_high, dz))
        if group == 3:
            return jnp.where(low_half(), row(mask_low, dz), row(mask_high, dz))
        return row(mask_own, dz)

    inner = both(0)
    if kz > 0:
        inner = jnp.where(rows8() < kz, both(1), inner)
    if kz < 0:
        inner = jnp.where(rows8() >= 8 + kz, both(-1), inner)
    return inner * CUT_SQ


def spread(first, second, lower, upper):
    lo = low_half()
    return [
        jnp.where(lo, lower, swap_halves(first)),
        swap_halves(jnp.where(lo, second, lower)),
        first,
        second,
        swap_halves(jnp.where(lo, upper, first)),
        jnp.where(lo, swap_halves(second), upper),
    ]


def add_pair(acc, mine, theirs, limit):
    away = [mine[k] - theirs[k] for k in range(3)]
    dist = away[0] * away[0] + away[1] * away[1] + away[2] * away[2]
    inside = (dist < limit) & (dist > 0.25)
    inv = lax.rsqrt(dist)
    inv_sq = inv * inv
    inv_six = inv_sq * inv_sq * inv_sq
    weight = inv_sq * (inv_six * (48.0 * inv_six - 24.0)) - SHIFT_FORCE * inv
    weight = jnp.where(inside, weight, 0.0)
    for k in range(3):
        term = weight * away[k]
        acc[k] = term if acc[k] is None else acc[k] + term


def in_range(*steps):
    return sum(abs(step) == 2 for step in steps) < 2


def row_frame(parts):
    row = rows8()
    total, above, below = parts.get(0), None, None
    for kz, part in parts.items():
        if kz == 0:
            continue
        back = pltpu.roll(part, (8 - kz) % 8, 0)
        stays = row < 8 - kz if kz > 0 else row >= -kz
        kept, passed = jnp.where(stays, back, 0.0), jnp.where(stays, 0.0, back)
        total = kept if total is None else total + kept
        if kz > 0:
            above = passed if above is None else above + passed
        else:
            below = passed if below is None else below + passed
    if above is not None:
        total = total + from_cell_above(above)
    if below is not None:
        total = total + from_cell_below(below)
    return total


def add_pairs(frames, before, total, partner, limit, columns, rows):
    for kz in (-2, -1, 0, 1, 2):
        for x in range(4):
            for yy in range(2):
                mine = [frames[kz + 2, k, x, yy] for k in range(3)]
                acc = [None if before is None else before[kz + 2, k, x, yy] for k in range(3)]
                for kx in (-2, -1, 0, 1, 2):
                    for ky in (-2, -1, 0, 1, 2):
                        if not in_range(kx, ky, kz):
                            continue
                        if kx == 0 and ky == 0 and kz == 0:
                            continue
                        if x + kx not in columns or yy + ky + 2 not in rows:
                            continue
                        m = yy + ky + 2
                        add_pair(acc, mine, [partner(k, x + kx, m) for k in range(3)],
                                 limit(kz, (x + kx) // 4, m // 2))
                for k in range(3):
                    total[kz + 2, k, x, yy] = jnp.zeros((8, ATOMS), F32) if acc[k] is None else acc[k]


def own_kernel(own, mask, moved, frames, total, moved_out, sem):
    leaving = pltpu.make_async_copy(moved, moved_out, sem)
    leaving.start()
    row_frames(own, frames)
    table = {kz: limits(None, mask, None, kz, 0, 1) for kz in (-2, -1, 0, 1, 2)}
    add_pairs(frames, None, total, lambda k, x, m: own[k, x, m - 2], lambda kz, dx, g: table[kz],
              (0, 1, 2, 3), (2, 3))
    leaving.wait()


def relay_kernel(got_a, got_b, pay_a, pay_b):
    col_odd = (lax.axis_index("col") & 1) == 1
    lo = low_half()

    def pack(ref, near, far, offset):
        for k in range(3):
            for x in (near, far):
                from_a, from_b = got_a[k * 4 + x], got_b[k * 4 + x]
                if k == 0:
                    from_a, from_b = from_a + offset, from_b + offset
                lower = jnp.where(col_odd, from_b, from_a)
                upper = jnp.where(col_odd, from_a, from_b)
                ref[k, 0 if x == near else 2] = swap_halves(jnp.where(lo, upper, lower))
                if x == near:
                    ref[k, 1] = jnp.where(lo, lower, upper)

    def both(to_upper, to_lower):
        pack(to_upper, 3, 2, -CELL_XY)
        pack(to_lower, 0, 1, CELL_XY)

    by_parity(lax.axis_index("row"), both, pay_a, pay_b)


def column_kernel(own, mask, got_a, got_b, frames, total_in, total, table, near, outer):
    col_odd = (lax.axis_index("col") & 1) == 1
    for k in range(3):
        for x in range(4):
            from_a, from_b = got_a[k * 4 + x], got_b[k * 4 + x]
            lower = jnp.where(col_odd, from_b, from_a)
            upper = jnp.where(col_odd, from_a, from_b)
            six = spread(own[k, x, 0], own[k, x, 1], lower, upper)
            near[k, x, 0] = six[0]
            near[k, x, 1] = six[1]
            near[k, x, 2] = six[4]
            near[k, x, 3] = six[5]
    mask_a, mask_b = got_a[12:14], got_b[12:14]
    mask_low = jnp.where(col_odd, mask_b, mask_a)
    mask_high = jnp.where(col_odd, mask_a, mask_b)
    mask_own = mask[...]
    for kz in (-2, -1, 0, 1, 2):
        for n, dx in enumerate((-1, 1)):
            table[kz + 2, n, 0] = limits(mask_low, mask_own, mask_high, kz, dx, 1)
            table[kz + 2, n, 1] = limits(mask_low, mask_own, mask_high, kz, dx, 3)
        for g in (0, 2):
            outer[kz + 2, g // 2] = limits(mask_low, mask_own, mask_high, kz, 0, g)
    add_pairs(frames, total_in, total, lambda k, x, m: near[k, x, m if m < 2 else m - 2],
              lambda kz, dx, g: outer[kz + 2, g // 2], (0, 1, 2, 3), (0, 1, 4, 5))


def row_kernel(face_a, face_b, frames, total_in, table, base, side):
    row_odd = (lax.axis_index("row") & 1) == 1
    lo = low_half()
    for k in range(3):
        for n in range(2):
            first, second = face_a[k, n], face_b[k, n]
            for s in range(2):
                zero, one = [jnp.where(row_odd == (s == 0), second[yy], first[yy]) for yy in range(2)]
                side[s, k, n, 0] = zero
                side[s, k, n, 1] = one
                side[s, k, n, 2] = swap_halves(zero)
                side[s, k, n, 3] = swap_halves(one)
                side[s, k, n, 4] = swap_halves(jnp.where(lo, one, zero))

    for x in range(4):
        parts = [[{} for _ in range(3)] for _ in range(3)]
        for kz in (-2, -1, 0, 1, 2):
            mine = [[frames[kz + 2, k, x, yy] for k in range(3)] for yy in range(2)]
            inner = [jnp.where(lo, mine[1][k], mine[0][k]) for k in range(3)]
            acc = [[total_in[kz + 2, k, x, yy] for k in range(3)] for yy in range(2)]
            cross = [None] * 3
            for kx in (-2, -1, 1, 2):
                if 0 <= x + kx < 4:
                    continue
                s, n = (0, x + kx + 2) if kx < 0 else (1, x + kx - 4)
                limit = table[kz + 2, s, 0]
                for yy in range(2):
                    for i, ky in ((0, -yy), (1, 1 - yy), (2 + yy, 2)):
                        if in_range(kx, ky, kz):
                            add_pair(acc[yy], mine[yy], [side[s, k, n, i] for k in range(3)], limit)
                if in_range(kx, 1, kz):
                    add_pair(cross, inner, [side[s, k, n, 4] for k in range(3)], limit)
            for k in range(3):
                parts[0][k][kz], parts[1][k][kz] = acc[0][k], acc[1][k]
                if cross[k] is not None:
                    parts[2][k][kz] = cross[k]
        for k in range(3):
            zero, one, cross = [row_frame(parts[i][k]) for i in range(3)]
            base[k, x, 0] = zero + jnp.where(lo, 0.0, cross)
            base[k, x, 1] = one + jnp.where(lo, cross, 0.0)


def finish_kernel(got_a, got_b, frames, base, table, half, code, vel_out, frc_out, corner, new_vel, new_frc, sems):
    row_odd = (lax.axis_index("row") & 1) == 1
    lo = low_half()
    for k in range(3):
        for s in range(2):
            for i in range(3):
                corner[s, k, i] = jnp.where(row_odd == (s == 0), got_b[k, i], got_a[k, i])

    added = [[None] * 4 for _ in range(3)]
    for x in range(4):
        s, step = (0, -1) if x < 2 else (1, 1)
        edge = x in (0, 3)
        outer_parts, inner_parts = [{} for _ in range(3)], [{} for _ in range(3)]
        for kz in (-2, -1, 0, 1, 2):
            if abs(kz) == 2 and not edge:
                continue
            limit = table[kz + 2, s, 1]
            mine = [[frames[kz + 2, k, x, yy] for k in range(3)] for yy in range(2)]
            outer = [jnp.where(lo, mine[0][k], mine[1][k]) for k in range(3)]
            inner = [jnp.where(lo, mine[1][k], mine[0][k]) for k in range(3)]
            near, far, deep = [[corner[s, k, i] for k in range(3)] for i in range(3)]
            on_outer, on_inner = [None] * 3, [None] * 3
            if edge:
                add_pair(on_outer, outer, near, limit)
                if in_range(1, 2, kz):
                    add_pair(on_outer, outer, far, limit)
                    add_pair(on_inner, inner, near, limit)
            if in_range(2, 1, kz):
                add_pair(on_outer, outer, deep if edge else near, limit)
            for k in range(3):
                outer_parts[k][kz] = on_outer[k]
                if on_inner[k] is not None:
                    inner_parts[k][kz] = on_inner[k]
        for k in range(3):
            on_outer = row_frame(outer_parts[k])
            on_inner = row_frame(inner_parts[k]) if edge else 0.0
            added[k][x] = (on_outer, on_inner)

    copies = []
    for k in range(3):
        stacked = []
        for x in range(4):
            on_outer, on_inner = added[k][x]
            stacked.append(base[k, x, 0] + jnp.where(lo, on_outer, on_inner))
            stacked.append(base[k, x, 1] + jnp.where(lo, on_inner, on_outer))
        lattice = jnp.concatenate(stacked, axis=0)
        flipped = jnp.swapaxes(jnp.concatenate([lattice, lattice], axis=0), 0, 1)
        cells_first = jnp.where(lo[0:1], flipped[:CELLS], flipped[CELLS:])
        for g in range(8):
            rows = slice(g * 8, g * 8 + 8)
            value = lookup(cells_first[rows], code[rows, :])
            new_frc[k, rows, :] = value
            new_vel[k, rows, :] = half[k, rows, :] + (0.5 * TIME_STEP) * value
        leaving = [pltpu.make_async_copy(new_frc.at[k], frc_out.at[k], sems.at[k]),
                   pltpu.make_async_copy(new_vel.at[k], vel_out.at[k], sems.at[3 + k])]
        for copy in leaving:
            copy.start()
        copies += leaving
    for copy in copies:
        copy.wait()


def kernel_call(body, outs, args, specs=None, outs_specs=None, scratch=(), flops=0, name=None):
    moved = sum(4 * a.size for a in args) + sum(4 * s.size for s in outs)
    return pl.pallas_call(
        body,
        out_shape=outs,
        in_specs=[VMEM] * len(args) if specs is None else specs,
        out_specs=[VMEM] * len(outs) if outs_specs is None else outs_specs,
        scratch_shapes=list(scratch),
        compiler_params=pltpu.CompilerParams(vmem_limit_bytes=8 << 20),
        cost_estimate=pl.CostEstimate(flops=flops, bytes_accessed=moved, transcendentals=0),
        name=name,
    )(*args)


def pairing(count, odd):
    if odd:
        return [(i, (i + 1) % count if i % 2 else (i - 1) % count) for i in range(count)]
    return [(i, i ^ 1) for i in range(count)]


def exchange(first, second, axis):
    count = lax.axis_size(axis)
    return (lax.ppermute(first, axis, pairing(count, True)), lax.ppermute(second, axis, pairing(count, False)))


def per_device(positions, velocities, forces, tiles, counts):
    blocks, _, atoms = positions.shape
    assert blocks == CELLS and atoms == ATOMS
    row_count, col_count = lax.axis_size("row"), lax.axis_size("col")
    assert row_count % 2 == 0 and col_count % 2 == 0 and min(row_count, col_count) > 2
    by_component = [jnp.transpose(a, (1, 0, 2)) for a in (positions, velocities, forces)]
    tile_rows = jnp.transpose(tiles[0, 0], (1, 0))

    def f32(*shape):
        return jax.ShapeDtypeStruct(shape, F32)

    span = f32(3, CELLS, ATOMS)
    lattice = f32(3, 4, 2, 8, ATOMS)
    sums = f32(5, 3, 4, 2, 8, ATOMS)
    moved, half, code, own, mask, pay_a, pay_b, face_a, face_b = kernel_call(
        functools.partial(prepare_kernel, row_count, col_count),
        [span, span, jax.ShapeDtypeStruct((CELLS, ATOMS), jnp.int32), lattice, f32(2, 8, ATOMS),
         f32(14, 8, ATOMS), f32(14, 8, ATOMS), f32(3, 2, 2, 8, ATOMS), f32(3, 2, 2, 8, ATOMS)],
        [*(pltpu.with_memory_space_constraint(a, pltpu.HBM) for a in (*by_component, tile_rows)), counts],
        specs=[HBM, HBM, HBM, HBM, SMEM], name="prepare",
        scratch=[pltpu.VMEM(span.shape, F32)] * 3
        + [pltpu.VMEM(tile_rows.shape, jnp.int32), pltpu.SemaphoreType.DMA((10,))],
    )
    got_a, got_b = exchange(pay_a, pay_b, "col")
    face_a, face_b = exchange(face_a, face_b, "row")
    frames, total, moved = kernel_call(own_kernel, [sums, sums, span], [own, mask, moved], flops=10**8, name="own",
                                       outs_specs=[VMEM, VMEM, HBM], scratch=[pltpu.SemaphoreType.DMA])
    far_a, far_b = exchange(
        *kernel_call(relay_kernel, [f32(3, 3, 8, ATOMS)] * 2, [got_a, got_b], name="relay"), "row"
    )
    total, table = kernel_call(
        column_kernel, [sums, f32(5, 2, 2, 8, ATOMS)],
        [own, mask, got_a, got_b, frames, total], flops=10**8, name="column",
        scratch=[pltpu.VMEM((3, 4, 4, 8, ATOMS), F32), pltpu.VMEM((5, 2, 8, ATOMS), F32)],
    )
    (base,) = kernel_call(
        row_kernel, [lattice], [face_a, face_b, frames, total, table], flops=10**8, name="rows",
        scratch=[pltpu.VMEM((2, 3, 2, 5, 8, ATOMS), F32)],
    )
    new_vel, new_frc = kernel_call(
        finish_kernel, [span, span], [far_a, far_b, frames, base, table, half, code], flops=10**8,
        name="finish", outs_specs=[HBM, HBM],
        scratch=[pltpu.VMEM((2, 3, 3, 8, ATOMS), F32), pltpu.VMEM(span.shape, F32), pltpu.VMEM(span.shape, F32),
                 pltpu.SemaphoreType.DMA((6,))],
    )
    return tuple(jnp.transpose(a, (1, 0, 2)) for a in (moved, new_vel, new_frc))


def solution(mesh):
    in_specs = (
        P(("row", "col"), None, None),
        P(("row", "col"), None, None),
        P(("row", "col"), None, None),
        P("row", "col", None, None),
        P("row", "col"),
    )
    out_specs = (
        P(("row", "col"), None, None),
        P(("row", "col"), None, None),
        P(("row", "col"), None, None),
    )
    return jax.shard_map(
        per_device, mesh=mesh, in_specs=in_specs, out_specs=out_specs, check_vma=False
    )
```

time: 22 us -> 18.3 us (0.83)
  waiting for transfers between devices: 4 us -> 0.7 us
  local copies, waits for them, and re-layouts: 2.71 us -> 0 us
  starting transfers between devices: 8.22 us -> 10.2 us
  Pallas kernels: 5.5 us -> 5.8 us
    unnamed x8 -> x0, local copies, waits for them, and re-layouts: 2.71 us -> none
    ppermute x2 -> x3, waiting for transfers between devices: 2.5 us -> 0.01 us  [exchange(): lax.ppermute(first, axis, pairing(count, True))]
    ppermute x2 -> x3, starting transfers between devices: 7.69 us -> 9.16 us  [exchange(): lax.ppermute(first, axis, pairing(count, True))]
    ppermute x2 -> x3, waiting for transfers between devices: 1.5 us -> 0.69 us  [exchange(): lax.ppermute(second, axis, pairing(count, False))]
    ppermute x2 -> x3, starting transfers between devices: 0.53 us -> 1.07 us  [exchange(): lax.ppermute(second, axis, pairing(count, False))]
    pallas_call x5 -> x6, Pallas kernels: 5.5 us -> 5.8 us  [kernel_call(): pl.pallas_call(body, out_shape=outs, in_specs=[VMEM] * len(args) if specs...]
  transfers between devices with their start and end apart: 4 -> 6, of which waited for: 3 -> 1; matrix products, arithmetic and copies ran while one was open for 0% -> 0% of each run, Pallas kernels for 9% -> 15%
where the time goes in v1:
time: 18.3 us; the launch traced here: 18.1 us
  starting transfers between devices  10.2 us (56%)
  Pallas kernels  5.8 us (32%)
  between operations  1.33 us (7%)
  waiting for transfers between devices  0.7 us (4%)
    ppermute x3, starting transfers between devices, exchange(): lax.ppermute(first, axis, pairing(count, True))  9.16 us
    pallas_call x6, Pallas kernels, kernel_call(): pl.pallas_call(body, out_shape=outs, in_specs=[VMEM] * len(args) if specs...  5.8 us
    ppermute x3, starting transfers between devices, exchange(): lax.ppermute(second, axis, pairing(count, False))  1.07 us
    ppermute x3, waiting for transfers between devices, exchange(): lax.ppermute(second, axis, pairing(count, False))  0.69 us
  transfers between devices with their start and end apart: 6, of which 1 were waited for; matrix products, arithmetic and copies ran while one was open for 0% of the time, Pallas kernels for 15%

profile of v1, /device:TPU:0, one launch (start us, length us, event | category | flops | bytes accessed | tf_op | source)
XLA Modules:
  0.0 18.1 jit_solution(10933002369153119019)
XLA Ops:
  1.3 1.8 %prepare.1 = (f32[3,64,128]{2,1,0:T(8,128)S(1)}, f32[3,64,128]{2,1,0:T(8,128)S(1)}, s32[64,128]{1,0:T(8,128)S(1)}, f32[3,4,2,8,128]{4,3,2,1,0:T(8,128)S(1)}, f32...) custom-call(f32[3,64,128]{2,1,0:T(8,128)} %bitcast.9, ...), custom_call_target="tpu_custom_call" | custom-call | bytes 851972 | tf_op jit(solution)/shard_map/prepare/pallas_call | solution.py:450
  3.0 4.6 %collective-permute-start = (f32[14,8,128]{2,1,0:T(8,128)S(1)}, f32[14,8,128]{2,1,0:T(8,128)S(1)}, u32[]{:S(2)}, u32[]{:S(2)}) collective-permute-start(f32[14,8,128]{2,1,0:T(8,128)S(1)} %get-tuple-element.25), channel_id=1, source_target_pairs={{0,7},{1,2},{2,1},{3,4},{4,3},{5,6},{6,5},{7,0},{8,15},{9,10},{10,... | collective-permute-start | bytes 172040 | tf_op jit(solution)/shard_map/ppermute | solution.py:470
  7.6 0.0 collective-permute-start.1
  7.6 2.4 %collective-permute-start.4 = (f32[3,2,2,8,128]{4,3,2,1,0:T(8,128)S(1)}, f32[3,2,2,8,128]{4,3,2,1,0:T(8,128)S(1)}, u32[]{:S(2)}, u32[]{:S(2)}) collective-permute-start(f32[3,2,2,8,128]{4,3,2,1,0:T(8,128)S(1)} %get-tuple-element.30), channel_id=1, source_target_pairs={{0,24},{8,16},{16,8},{24,0},{1,25},{9,17},{17,9},{25,1},{2,26},{10... | collective-permute-start | bytes 147464 | tf_op jit(solution)/shard_map/ppermute | solution.py:470
  10.1 0.5 %collective-permute-start.5 = (f32[3,2,2,8,128]{4,3,2,1,0:T(8,128)S(1)}, f32[3,2,2,8,128]{4,3,2,1,0:T(8,128)S(1)}, u32[]{:S(2)}, u32[]{:S(2)}) collective-permute-start(f32[3,2,2,8,128]{4,3,2,1,0:T(8,128)S(1)} %get-tuple-element.31), channel_id=1, source_target_pairs={{0,8},{8,0},{16,24},{24,16},{1,9},{9,1},{17,25},{25,17},{2,10},{10... | collective-permute-start | bytes 147464 | tf_op jit(solution)/shard_map/ppermute | solution.py:470
  10.6 0.0 collective-permute-done.got_a
  10.6 0.0 collective-permute-done.1.got_b
  10.6 0.1 relay.1
  10.7 2.1 %collective-permute-start.2 = (f32[3,3,8,128]{3,2,1,0:T(8,128)S(1)}, f32[3,3,8,128]{3,2,1,0:T(8,128)S(1)}, u32[]{:S(2)}, u32[]{:S(2)}) collective-permute-start(f32[3,3,8,128]{3,2,1,0:T(8,128)S(1)} %get-tuple-element.27), channel_id=1, source_target_pairs={{0,24},{8,16},{16,8},{24,0},{1,25},{9,17},{17,9},{25,1},{2,26},{10... | collective-permute-start | bytes 110600 | tf_op jit(solution)/shard_map/ppermute | solution.py:470
  12.8 0.5 %collective-permute-start.3 = (f32[3,3,8,128]{3,2,1,0:T(8,128)S(1)}, f32[3,3,8,128]{3,2,1,0:T(8,128)S(1)}, u32[]{:S(2)}, u32[]{:S(2)}) collective-permute-start(f32[3,3,8,128]{3,2,1,0:T(8,128)S(1)} %get-tuple-element.28), channel_id=1, source_target_pairs={{0,8},{8,0},{16,24},{24,16},{1,9},{9,1},{17,25},{25,17},{2,10},{10... | collective-permute-start | bytes 110600 | tf_op jit(solution)/shard_map/ppermute | solution.py:470
  13.4 1.0 %own.1 = (f32[5,3,4,2,8,128]{5,4,3,2,1,0:T(8,128)S(1)}, f32[5,3,4,2,8,128]{5,4,3,2,1,0:T(8,128)S(1)}, f32[3,64,128]{2,1,0:T(8,128)}) custom-call(f32[3,4,2,8,128]{4,3,2,1,0:T(8,128)S(1)} %get-tuple-element.21.own, f32[2,8,128]{2,1,0:T(8,128)S(1)} %get-tuple-element.22.mask, f32[3,64,128]{2,1,0:T(8,128)S(1)} %get-tuple-element.23.moved), custom_call_target="tpu_custom_call" | custom-call | flops 100000000 | bytes 1286144 | tf_op jit(solution)/shard_map/own/pallas_call | solution.py:450
  14.4 1.0 %column.1 = (f32[5,3,4,2,8,128]{5,4,3,2,1,0:T(8,128)S(1)}, f32[5,2,2,8,128]{4,3,2,1,0:T(8,128)S(1)}) custom-call(f32[3,4,2,8,128]{4,3,2,1,0:T(8,128)S(1)} %get-tuple-element.21.own, f32[2,8,128]{2,1,0:T(8,128)S(1)} %get-tuple-element.22.mask, f32[14,8,128]{2,1,0:T(8,128)S(1)} %collective-permute-done.got_a, f32[14,8,128]{2,1,0:T(8,128)S(1)} %collective-permute-done.1.got_b, ...), custom_call_target="tpu_custom_call" | custom-call | flops 100000000 | bytes 1777664 | tf_op jit(solution)/shard_map/column/pallas_call | solution.py:450
  15.4 0.0 collective-permute-done.4.face_a
  15.5 0.0 collective-permute-done.5.face_b
  15.5 0.6 %rows.1.base = f32[3,4,2,8,128]{4,3,2,1,0:T(8,128)S(1)} custom-call(f32[3,2,2,8,128]{4,3,2,1,0:T(8,128)S(1)} %collective-permute-done.4.face_a, f32[3,2,2,8,128]{4,3,2,1,0:T(8,128)S(1)} %collective-permute-done.5.face_b, f32[5,3,4,2,8,128]{5,4,3,2,1,0:T(8,128)S(1)} %get-tuple-element.29.frames, f32[5,3,4,2,8,128]{5,4,3,2,1,0:T(8,128)S(1)} %get-tuple-element.33.total_in, ...), custom_call_target="tpu_custom_call" | custom-call | flops 100000000 | bytes 1261568 | tf_op jit(solution)/shard_map/rows/pallas_call | solution.py:450
  16.1 0.0 collective-permute-done.2.got_a
  16.1 0.7 %collective-permute-done.3.got_b = f32[3,3,8,128]{3,2,1,0:T(8,128)S(1)} collective-permute-done((f32[3,3,8,128]{3,2,1,0:T(8,128)S(1)}, f32[3,3,8,128]{3,2,1,0:T(8,128)S(1)}, u32[]{:S(2)}, u32[]{:S(2)}) %collective-permute-start.3) | collective-permute-done | bytes 36896 | tf_op jit(solution)/shard_map/ppermute | solution.py:470
  16.8 1.3 %finish.1 = (f32[3,64,128]{2,1,0:T(8,128)}, f32[3,64,128]{2,1,0:T(8,128)}) custom-call(f32[3,3,8,128]{3,2,1,0:T(8,128)S(1)} %collective-permute-done.2.got_a, f32[3,3,8,128]{3,2,1,0:T(8,128)S(1)} %collective-permute-done.3.got_b, f32[5,3,4,2,8,128]{5,4,3,2,1,0:T(8,128)S(1)} %get-tuple-element.29.frames, f32[3,4,2,8,128]{4,3,2,1,0:T(8,128)S(1)} %rows.1.base, ...), custom_call_target="tpu_custom_call" | custom-call | flops 100000000 | bytes 1073152 | tf_op jit(solution)/shard_map/finish/pallas_call | solution.py:450
Async XLA Ops:
  3.0 7.6 %collective-permute-start = (f32[14,8,128]{2,1,0:T(8,128)S(1)}, f32[14,8,128]{2,1,0:T(8,128)S(1)}, u32[]{:S(2)}, u32[]{:S(2)}) collective-permute-start(f32[14,8,128]{2,1,0:T(8,128)S(1)} %get-tuple-element.25), channel_id=1, source_target_pairs={{0,7},{1,2},{2,1},{3,4},{4,3},{5,6},{6,5},{7,0},{8,15},{9,10},{10,... | collective-permute-start | bytes 172040 | tf_op jit(solution)/shard_map/ppermute | solution.py:470
  7.6 3.0 %collective-permute-start.1 = (f32[14,8,128]{2,1,0:T(8,128)S(1)}, f32[14,8,128]{2,1,0:T(8,128)S(1)}, u32[]{:S(2)}, u32[]{:S(2)}) collective-permute-start(f32[14,8,128]{2,1,0:T(8,128)S(1)} %get-tuple-element.26), channel_id=1, source_target_pairs={{0,1},{1,0},{2,3},{3,2},{4,5},{5,4},{6,7},{7,6},{8,9},{9,8},{10,11... | collective-permute-start | bytes 172040 | tf_op jit(solution)/shard_map/ppermute | solution.py:470
  7.6 7.8 %collective-permute-start.4 = (f32[3,2,2,8,128]{4,3,2,1,0:T(8,128)S(1)}, f32[3,2,2,8,128]{4,3,2,1,0:T(8,128)S(1)}, u32[]{:S(2)}, u32[]{:S(2)}) collective-permute-start(f32[3,2,2,8,128]{4,3,2,1,0:T(8,128)S(1)} %get-tuple-element.30), channel_id=1, source_target_pairs={{0,24},{8,16},{16,8},{24,0},{1,25},{9,17},{17,9},{25,1},{2,26},{10... | collective-permute-start | bytes 147464 | tf_op jit(solution)/shard_map/ppermute | solution.py:470
  10.1 5.4 %collective-permute-start.5 = (f32[3,2,2,8,128]{4,3,2,1,0:T(8,128)S(1)}, f32[3,2,2,8,128]{4,3,2,1,0:T(8,128)S(1)}, u32[]{:S(2)}, u32[]{:S(2)}) collective-permute-start(f32[3,2,2,8,128]{4,3,2,1,0:T(8,128)S(1)} %get-tuple-element.31), channel_id=1, source_target_pairs={{0,8},{8,0},{16,24},{24,16},{1,9},{9,1},{17,25},{25,17},{2,10},{10... | collective-permute-start | bytes 147464 | tf_op jit(solution)/shard_map/ppermute | solution.py:470
  10.7 5.4 %collective-permute-start.2 = (f32[3,3,8,128]{3,2,1,0:T(8,128)S(1)}, f32[3,3,8,128]{3,2,1,0:T(8,128)S(1)}, u32[]{:S(2)}, u32[]{:S(2)}) collective-permute-start(f32[3,3,8,128]{3,2,1,0:T(8,128)S(1)} %get-tuple-element.27), channel_id=1, source_target_pairs={{0,24},{8,16},{16,8},{24,0},{1,25},{9,17},{17,9},{25,1},{2,26},{10... | collective-permute-start | bytes 110600 | tf_op jit(solution)/shard_map/ppermute | solution.py:470
  12.8 4.0 %collective-permute-start.3 = (f32[3,3,8,128]{3,2,1,0:T(8,128)S(1)}, f32[3,3,8,128]{3,2,1,0:T(8,128)S(1)}, u32[]{:S(2)}, u32[]{:S(2)}) collective-permute-start(f32[3,3,8,128]{3,2,1,0:T(8,128)S(1)} %get-tuple-element.28), channel_id=1, source_target_pairs={{0,8},{8,0},{16,24},{24,16},{1,9},{9,1},{17,25},{25,17},{2,10},{10... | collective-permute-start | bytes 110600 | tf_op jit(solution)/shard_map/ppermute | solution.py:470

commit v2 on v1

--- a/solution.py
+++ b/solution.py
@@ -165,7 +165,7 @@
                     to_lower[k, n, yy] = down + CELL_XY if k == 0 else down
 
     by_parity(my_col, pack, pay_a, pay_b)
-    by_parity(my_row, pack_faces, face_a, face_b)
+    pack_faces(face_a, face_b)
 
 
 def row_frames(own, frames):
@@ -304,7 +304,7 @@
                     from_a, from_b = from_a + offset, from_b + offset
                 lower = jnp.where(col_odd, from_b, from_a)
                 upper = jnp.where(col_odd, from_a, from_b)
-                ref[k, 0 if x == near else 2] = swap_halves(jnp.where(lo, upper, lower))
+                ref[k, 0 if x == near else 2] = jnp.where(lo, upper, lower)
                 if x == near:
                     ref[k, 1] = jnp.where(lo, lower, upper)
 
@@ -312,7 +312,7 @@
         pack(to_upper, 3, 2, -CELL_XY)
         pack(to_lower, 0, 1, CELL_XY)
 
-    by_parity(lax.axis_index("row"), both, pay_a, pay_b)
+    both(pay_a, pay_b)
 
 
 def column_kernel(own, mask, got_a, got_b, frames, total_in, total, table, near, outer):
@@ -342,13 +342,12 @@
 
 
 def row_kernel(face_a, face_b, frames, total_in, table, base, side):
-    row_odd = (lax.axis_index("row") & 1) == 1
     lo = low_half()
     for k in range(3):
         for n in range(2):
             first, second = face_a[k, n], face_b[k, n]
             for s in range(2):
-                zero, one = [jnp.where(row_odd == (s == 0), second[yy], first[yy]) for yy in range(2)]
+                zero, one = [(second if s == 0 else first)[yy] for yy in range(2)]
                 side[s, k, n, 0] = zero
                 side[s, k, n, 1] = one
                 side[s, k, n, 2] = swap_halves(zero)
@@ -383,52 +382,48 @@
             base[k, x, 1] = one + jnp.where(lo, cross, 0.0)
 
 
-def finish_kernel(got_a, got_b, frames, base, table, half, code, vel_out, frc_out, corner, new_vel, new_frc, sems):
-    row_odd = (lax.axis_index("row") & 1) == 1
+def add_corners(got, frames, table, base, total, upper):
     lo = low_half()
-    for k in range(3):
-        for s in range(2):
-            for i in range(3):
-                corner[s, k, i] = jnp.where(row_odd == (s == 0), got_b[k, i], got_a[k, i])
-
-    added = [[None] * 4 for _ in range(3)]
-    for x in range(4):
-        s, step = (0, -1) if x < 2 else (1, 1)
-        edge = x in (0, 3)
-        outer_parts, inner_parts = [{} for _ in range(3)], [{} for _ in range(3)]
-        for kz in (-2, -1, 0, 1, 2):
-            if abs(kz) == 2 and not edge:
-                continue
-            limit = table[kz + 2, s, 1]
-            mine = [[frames[kz + 2, k, x, yy] for k in range(3)] for yy in range(2)]
-            outer = [jnp.where(lo, mine[0][k], mine[1][k]) for k in range(3)]
-            inner = [jnp.where(lo, mine[1][k], mine[0][k]) for k in range(3)]
-            near, far, deep = [[corner[s, k, i] for k in range(3)] for i in range(3)]
-            on_outer, on_inner = [None] * 3, [None] * 3
-            if edge:
-                add_pair(on_outer, outer, near, limit)
-                if in_range(1, 2, kz):
-                    add_pair(on_outer, outer, far, limit)
-                    add_pair(on_inner, inner, near, limit)
-            if in_range(2, 1, kz):
-                add_pair(on_outer, outer, deep if edge else near, limit)
-            for k in range(3):
-                outer_parts[k][kz] = on_outer[k]
-                if on_inner[k] is not None:
-                    inner_parts[k][kz] = on_inner[k]
+    side, edge, inset = (1, 3, 2) if upper else (0, 0, 1)
+    near, deep = [[swap_halves(got[k, i]) for k in range(3)] for i in (0, 2)]
+    far = [got[k, 1] for k in range(3)]
+    outer_parts, inner_parts, inset_parts = [[{} for _ in range(3)] for _ in range(3)]
+    for kz in (-2, -1, 0, 1, 2):
+        limit = table[kz + 2, side, 1]
+        mine = [[frames[kz + 2, k, edge, yy] for k in range(3)] for yy in range(2)]
+        outer = [jnp.where(lo, mine[0][k], mine[1][k]) for k in range(3)]
+        inner = [jnp.where(lo, mine[1][k], mine[0][k]) for k in range(3)]
+        on_outer, on_inner, on_inset = [None] * 3, [None] * 3, [None] * 3
+        add_pair(on_outer, outer, near, limit)
+        if in_range(1, 2, kz):
+            add_pair(on_outer, outer, far, limit)
+            add_pair(on_inner, inner, near, limit)
+            add_pair(on_outer, outer, deep, limit)
+            mine = [[frames[kz + 2, k, inset, yy] for k in range(3)] for yy in range(2)]
+            add_pair(on_inset, [jnp.where(lo, mine[0][k], mine[1][k]) for k in range(3)], near, limit)
         for k in range(3):
-            on_outer = row_frame(outer_parts[k])
-            on_inner = row_frame(inner_parts[k]) if edge else 0.0
-            added[k][x] = (on_outer, on_inner)
-
+            outer_parts[k][kz] = on_outer[k]
+            if on_inner[k] is not None:
+                inner_parts[k][kz], inset_parts[k][kz] = on_inner[k], on_inset[k]
+    total[...] = base[...]
+    for k in range(3):
+        on_outer, on_inner, on_inset = row_frame(outer_parts[k]), row_frame(inner_parts[k]), row_frame(inset_parts[k])
+        total[k, edge, 0] = base[k, edge, 0] + jnp.where(lo, on_outer, on_inner)
+        total[k, edge, 1] = base[k, edge, 1] + jnp.where(lo, on_inner, on_outer)
+        total[k, inset, 0] = base[k, inset, 0] + jnp.where(lo, on_inset, 0.0)
+        total[k, inset, 1] = base[k, inset, 1] + jnp.where(lo, 0.0, on_inset)
+
+
+def first_corner_kernel(got, frames, table, base, total):
+    add_corners(got, frames, table, base, total, False)
+
+
+def finish_kernel(got, frames, table, base, half, code, vel_out, frc_out, total, new_vel, new_frc, sems):
+    add_corners(got, frames, table, base, total, True)
+    lo = low_half()
     copies = []
     for k in range(3):
-        stacked = []
-        for x in range(4):
-            on_outer, on_inner = added[k][x]
-            stacked.append(base[k, x, 0] + jnp.where(lo, on_outer, on_inner))
-            stacked.append(base[k, x, 1] + jnp.where(lo, on_inner, on_outer))
-        lattice = jnp.concatenate(stacked, axis=0)
+        lattice = total[k].reshape(CELLS, ATOMS)
         flipped = jnp.swapaxes(jnp.concatenate([lattice, lattice], axis=0), 0, 1)
         cells_first = jnp.where(lo[0:1], flipped[:CELLS], flipped[CELLS:])
         for g in range(8):
@@ -470,6 +465,14 @@
     return (lax.ppermute(first, axis, pairing(count, True)), lax.ppermute(second, axis, pairing(count, False)))
 
 
+def pass_round(first, second, axis):
+    count = lax.axis_size(axis)
+    up = [(i, (i + 1) % count) for i in range(count)]
+    down = [(target, source) for source, target in up]
+    from_lower = lax.ppermute(first, axis, up)
+    return lax.ppermute(second, axis, down), from_lower
+
+
 def per_device(positions, velocities, forces, tiles, counts):
     blocks, _, atoms = positions.shape
     assert blocks == CELLS and atoms == ATOMS
@@ -494,10 +497,10 @@
         + [pltpu.VMEM(tile_rows.shape, jnp.int32), pltpu.SemaphoreType.DMA((10,))],
     )
     got_a, got_b = exchange(pay_a, pay_b, "col")
-    face_a, face_b = exchange(face_a, face_b, "row")
+    face_a, face_b = pass_round(face_a, face_b, "row")
     frames, total, moved = kernel_call(own_kernel, [sums, sums, span], [own, mask, moved], flops=10**8, name="own",
                                        outs_specs=[VMEM, VMEM, HBM], scratch=[pltpu.SemaphoreType.DMA])
-    far_a, far_b = exchange(
+    far_a, far_b = pass_round(
         *kernel_call(relay_kernel, [f32(3, 3, 8, ATOMS)] * 2, [got_a, got_b], name="relay"), "row"
     )
     total, table = kernel_call(
@@ -509,10 +512,11 @@
         row_kernel, [lattice], [face_a, face_b, frames, total, table], flops=10**8, name="rows",
         scratch=[pltpu.VMEM((2, 3, 2, 5, 8, ATOMS), F32)],
     )
+    (base,) = kernel_call(first_corner_kernel, [lattice], [far_b, frames, table, base], flops=10**7, name="corners")
     new_vel, new_frc = kernel_call(
-        finish_kernel, [span, span], [far_a, far_b, frames, base, table, half, code], flops=10**8,
+        finish_kernel, [span, span], [far_a, frames, table, base, half, code], flops=10**8,
         name="finish", outs_specs=[HBM, HBM],
-        scratch=[pltpu.VMEM((2, 3, 3, 8, ATOMS), F32), pltpu.VMEM(span.shape, F32), pltpu.VMEM(span.shape, F32),
+        scratch=[pltpu.VMEM(lattice.shape, F32), pltpu.VMEM(span.shape, F32), pltpu.VMEM(span.shape, F32),
                  pltpu.SemaphoreType.DMA((6,))],
     )
     return tuple(jnp.transpose(a, (1, 0, 2)) for a in (moved, new_vel, new_frc))

time: 18.3 us -> 17.6 us (0.962)
  waiting for transfers between devices: 0.7 us -> 0.06 us
    ppermute x0 -> x4, starting transfers between devices: none -> 5.48 us  [the longest x2 3.47 us: pass_round(): return (lax.ppermute(second, axis, down), from_lower)]
    ppermute x3 -> x1, starting transfers between devices: 9.16 us -> 4.57 us  [exchange(): lax.ppermute(first, axis, pairing(count, True))]
    ppermute x3 -> x1, starting transfers between devices: 1.07 us -> 0.01 us  [exchange(): lax.ppermute(second, axis, pairing(count, False))]
    ppermute x3 -> x1, waiting for transfers between devices: 0.69 us -> 0.01 us  [exchange(): lax.ppermute(second, axis, pairing(count, False))]
    pallas_call x6 -> x7, Pallas kernels: 5.8 us -> 5.94 us  [kernel_call(): pl.pallas_call(body, out_shape=outs, in_specs=[VMEM] * len(args) if specs...]
  transfers between devices with their start and end apart: 6 -> 6, of which waited for: 1 -> 0; matrix products, arithmetic and copies ran while one was open for 0% -> 0% of each run, Pallas kernels for 15% -> 17%
where the time goes in v2:
time: 17.6 us; the launch traced here: 17.4 us
  starting transfers between devices  10.1 us (57%)
  Pallas kernels  5.94 us (34%)
  between operations  1.34 us (8%)
    pallas_call x7, Pallas kernels, kernel_call(): pl.pallas_call(body, out_shape=outs, in_specs=[VMEM] * len(args) if specs...  5.94 us
    ppermute x1, starting transfers between devices, exchange(): lax.ppermute(first, axis, pairing(count, True))  4.57 us
    ppermute x2, starting transfers between devices, pass_round(): return (lax.ppermute(second, axis, down), from_lower)  3.47 us
    ppermute x2, starting transfers between devices, pass_round(): from_lower = lax.ppermute(first, axis, up)  2.01 us
  transfers between devices with their start and end apart: 6, of which 0 were waited for; matrix products, arithmetic and copies ran while one was open for 0% of the time, Pallas kernels for 17%

profile of v2, /device:TPU:0, one launch (start us, length us, event | category | flops | bytes accessed | tf_op | source)
XLA Modules:
  0.0 17.4 jit_solution(6189999499204854556)
XLA Ops:
  1.3 1.8 %prepare.1 = (f32[3,64,128]{2,1,0:T(8,128)S(1)}, f32[3,64,128]{2,1,0:T(8,128)S(1)}, s32[64,128]{1,0:T(8,128)S(1)}, f32[3,4,2,8,128]{4,3,2,1,0:T(8,128)S(1)}, f32...) custom-call(f32[3,64,128]{2,1,0:T(8,128)} %bitcast.9, ...), custom_call_target="tpu_custom_call" | custom-call | bytes 851972 | tf_op jit(solution)/shard_map/prepare/pallas_call | solution.py:445
  3.0 4.6 %collective-permute-start = (f32[14,8,128]{2,1,0:T(8,128)S(1)}, f32[14,8,128]{2,1,0:T(8,128)S(1)}, u32[]{:S(2)}, u32[]{:S(2)}) collective-permute-start(f32[14,8,128]{2,1,0:T(8,128)S(1)} %get-tuple-element.25), channel_id=1, source_target_pairs={{0,7},{1,2},{2,1},{3,4},{4,3},{5,6},{6,5},{7,0},{8,15},{9,10},{10,... | collective-permute-start | bytes 172040 | tf_op jit(solution)/shard_map/ppermute | solution.py:465
  7.6 0.0 collective-permute-start.1
  7.6 2.4 %collective-permute-start.4 = (f32[3,2,2,8,128]{4,3,2,1,0:T(8,128)S(1)}, f32[3,2,2,8,128]{4,3,2,1,0:T(8,128)S(1)}, u32[]{:S(2)}, u32[]{:S(2)}) collective-permute-start(f32[3,2,2,8,128]{4,3,2,1,0:T(8,128)S(1)} %get-tuple-element.32), channel_id=1, source_target_pairs={{8,0},{16,8},{24,16},{0,24},{9,1},{17,9},{25,17},{1,25},{10,2},{18... | collective-permute-start | bytes 147464 | tf_op jit(solution)/shard_map/ppermute | solution.py:473
  10.1 0.0 collective-permute-start.5
  10.1 0.0 collective-permute-done.got_a
  10.1 0.0 collective-permute-done.1.got_b
  10.1 2.0 %collective-permute-start.3 = (f32[3,3,8,128]{3,2,1,0:T(8,128)S(1)}, f32[3,3,8,128]{3,2,1,0:T(8,128)S(1)}, u32[]{:S(2)}, u32[]{:S(2)}) collective-permute-start(f32[3,3,8,128]{3,2,1,0:T(8,128)S(1)} %get-tuple-element.31), channel_id=1, source_target_pairs={{0,8},{8,16},{16,24},{24,0},{1,9},{9,17},{17,25},{25,1},{2,10},{10... | collective-permute-start | bytes 110600 | tf_op jit(solution)/shard_map/ppermute | solution.py:472
  12.1 1.0 %collective-permute-start.2 = (f32[3,3,8,128]{3,2,1,0:T(8,128)S(1)}, f32[3,3,8,128]{3,2,1,0:T(8,128)S(1)}, u32[]{:S(2)}, u32[]{:S(2)}) collective-permute-start(f32[3,3,8,128]{3,2,1,0:T(8,128)S(1)} %get-tuple-element.27), channel_id=1, source_target_pairs={{8,0},{16,8},{24,16},{0,24},{9,1},{17,9},{25,17},{1,25},{10,2},{18... | collective-permute-start | bytes 110600 | tf_op jit(solution)/shard_map/ppermute | solution.py:473
  13.1 1.0 %own.1 = (f32[5,3,4,2,8,128]{5,4,3,2,1,0:T(8,128)S(1)}, f32[5,3,4,2,8,128]{5,4,3,2,1,0:T(8,128)S(1)}, f32[3,64,128]{2,1,0:T(8,128)}) custom-call(f32[3,4,2,8,128]{4,3,2,1,0:T(8,128)S(1)} %get-tuple-element.21.own, f32[2,8,128]{2,1,0:T(8,128)S(1)} %get-tuple-element.22.mask, f32[3,64,128]{2,1,0:T(8,128)S(1)} %get-tuple-element.23.moved), custom_call_target="tpu_custom_call" | custom-call | flops 100000000 | bytes 1286144 | tf_op jit(solution)/shard_map/own/pallas_call | solution.py:445
  14.2 1.0 %column.1 = (f32[5,3,4,2,8,128]{5,4,3,2,1,0:T(8,128)S(1)}, f32[5,2,2,8,128]{4,3,2,1,0:T(8,128)S(1)}) custom-call(f32[3,4,2,8,128]{4,3,2,1,0:T(8,128)S(1)} %get-tuple-element.21.own, f32[2,8,128]{2,1,0:T(8,128)S(1)} %get-tuple-element.22.mask, f32[14,8,128]{2,1,0:T(8,128)S(1)} %collective-permute-done.got_a, f32[14,8,128]{2,1,0:T(8,128)S(1)} %collective-permute-done.1.got_b, ...), custom_call_target="tpu_custom_call" | custom-call | flops 100000000 | bytes 1777664 | tf_op jit(solution)/shard_map/column/pallas_call | solution.py:445
  15.2 0.0 collective-permute-done.4.face_a
  15.2 0.0 collective-permute-done.5.face_b
  15.2 0.7 %rows.1.base = f32[3,4,2,8,128]{4,3,2,1,0:T(8,128)S(1)} custom-call(f32[3,2,2,8,128]{4,3,2,1,0:T(8,128)S(1)} %collective-permute-done.4.face_a, f32[3,2,2,8,128]{4,3,2,1,0:T(8,128)S(1)} %collective-permute-done.5.face_b, f32[5,3,4,2,8,128]{5,4,3,2,1,0:T(8,128)S(1)} %get-tuple-element.28.frames, f32[5,3,4,2,8,128]{5,4,3,2,1,0:T(8,128)S(1)} %get-tuple-element.34.total_in, ...), custom_call_target="tpu_custom_call" | custom-call | flops 100000000 | bytes 1261568 | tf_op jit(solution)/shard_map/rows/pallas_call | solution.py:445
  15.9 0.0 collective-permute-done.3.got
  15.9 0.2 %corners.1.base = f32[3,4,2,8,128]{4,3,2,1,0:T(8,128)S(1)} custom-call(f32[3,3,8,128]{3,2,1,0:T(8,128)S(1)} %collective-permute-done.3.got, f32[5,3,4,2,8,128]{5,4,3,2,1,0:T(8,128)S(1)} %get-tuple-element.28.frames, f32[5,2,2,8,128]{4,3,2,1,0:T(8,128)S(1)} %get-tuple-element.30.table, f32[3,4,2,8,128]{4,3,2,1,0:T(8,128)S(1)} %rows.1.base), custom_call_target="tpu_custom_call" | custom-call | flops 10000000 | bytes 806912 | tf_op jit(solution)/shard_map/corners/pallas_call | solution.py:445
  16.1 0.0 collective-permute-done.2.got
  16.2 1.2 %finish.1 = (f32[3,64,128]{2,1,0:T(8,128)}, f32[3,64,128]{2,1,0:T(8,128)}) custom-call(f32[3,3,8,128]{3,2,1,0:T(8,128)S(1)} %collective-permute-done.2.got, f32[5,3,4,2,8,128]{5,4,3,2,1,0:T(8,128)S(1)} %get-tuple-element.28.frames, f32[5,2,2,8,128]{4,3,2,1,0:T(8,128)S(1)} %get-tuple-element.30.table, f32[3,4,2,8,128]{4,3,2,1,0:T(8,128)S(1)} %corners.1.base, ...), custom_call_target="tpu_custom_call" | custom-call | flops 100000000 | bytes 1036288 | tf_op jit(solution)/shard_map/finish/pallas_call | solution.py:445
  (1 shorter events, 0.0 us)
Async XLA Ops:
  3.0 7.0 %collective-permute-start = (f32[14,8,128]{2,1,0:T(8,128)S(1)}, f32[14,8,128]{2,1,0:T(8,128)S(1)}, u32[]{:S(2)}, u32[]{:S(2)}) collective-permute-start(f32[14,8,128]{2,1,0:T(8,128)S(1)} %get-tuple-element.25), channel_id=1, source_target_pairs={{0,7},{1,2},{2,1},{3,4},{4,3},{5,6},{6,5},{7,0},{8,15},{9,10},{10,... | collective-permute-start | bytes 172040 | tf_op jit(solution)/shard_map/ppermute | solution.py:465
  7.6 2.5 %collective-permute-start.1 = (f32[14,8,128]{2,1,0:T(8,128)S(1)}, f32[14,8,128]{2,1,0:T(8,128)S(1)}, u32[]{:S(2)}, u32[]{:S(2)}) collective-permute-start(f32[14,8,128]{2,1,0:T(8,128)S(1)} %get-tuple-element.26), channel_id=1, source_target_pairs={{0,1},{1,0},{2,3},{3,2},{4,5},{5,4},{6,7},{7,6},{8,9},{9,8},{10,11... | collective-permute-start | bytes 172040 | tf_op jit(solution)/shard_map/ppermute | solution.py:465
  7.6 7.6 %collective-permute-start.4 = (f32[3,2,2,8,128]{4,3,2,1,0:T(8,128)S(1)}, f32[3,2,2,8,128]{4,3,2,1,0:T(8,128)S(1)}, u32[]{:S(2)}, u32[]{:S(2)}) collective-permute-start(f32[3,2,2,8,128]{4,3,2,1,0:T(8,128)S(1)} %get-tuple-element.32), channel_id=1, source_target_pairs={{8,0},{16,8},{24,16},{0,24},{9,1},{17,9},{25,17},{1,25},{10,2},{18... | collective-permute-start | bytes 147464 | tf_op jit(solution)/shard_map/ppermute | solution.py:473
  10.1 5.2 %collective-permute-start.5 = (f32[3,2,2,8,128]{4,3,2,1,0:T(8,128)S(1)}, f32[3,2,2,8,128]{4,3,2,1,0:T(8,128)S(1)}, u32[]{:S(2)}, u32[]{:S(2)}) collective-permute-start(f32[3,2,2,8,128]{4,3,2,1,0:T(8,128)S(1)} %get-tuple-element.33), channel_id=1, source_target_pairs={{0,8},{8,16},{16,24},{24,0},{1,9},{9,17},{17,25},{25,1},{2,10},{10... | collective-permute-start | bytes 147464 | tf_op jit(solution)/shard_map/ppermute | solution.py:472
  10.1 5.8 %collective-permute-start.3 = (f32[3,3,8,128]{3,2,1,0:T(8,128)S(1)}, f32[3,3,8,128]{3,2,1,0:T(8,128)S(1)}, u32[]{:S(2)}, u32[]{:S(2)}) collective-permute-start(f32[3,3,8,128]{3,2,1,0:T(8,128)S(1)} %get-tuple-element.31), channel_id=1, source_target_pairs={{0,8},{8,16},{16,24},{24,0},{1,9},{9,17},{17,25},{25,1},{2,10},{10... | collective-permute-start | bytes 110600 | tf_op jit(solution)/shard_map/ppermute | solution.py:472
  12.1 4.0 %collective-permute-start.2 = (f32[3,3,8,128]{3,2,1,0:T(8,128)S(1)}, f32[3,3,8,128]{3,2,1,0:T(8,128)S(1)}, u32[]{:S(2)}, u32[]{:S(2)}) collective-permute-start(f32[3,3,8,128]{3,2,1,0:T(8,128)S(1)} %get-tuple-element.27), channel_id=1, source_target_pairs={{8,0},{16,8},{24,16},{0,24},{9,1},{17,9},{25,17},{1,25},{10,2},{18... | collective-permute-start | bytes 110600 | tf_op jit(solution)/shard_map/ppermute | solution.py:473

commit v3 on v2

--- a/solution.py
+++ b/solution.py
@@ -222,15 +222,22 @@
     ]
 
 
-def add_pair(acc, mine, theirs, limit):
+def pair_weight(mine, theirs):
     away = [mine[k] - theirs[k] for k in range(3)]
     dist = away[0] * away[0] + away[1] * away[1] + away[2] * away[2]
-    inside = (dist < limit) & (dist > 0.25)
     inv = lax.rsqrt(dist)
     inv_sq = inv * inv
     inv_six = inv_sq * inv_sq * inv_sq
-    weight = inv_sq * (inv_six * (48.0 * inv_six - 24.0)) - SHIFT_FORCE * inv
-    weight = jnp.where(inside, weight, 0.0)
+    return away, inv_sq * (inv_six * (48.0 * inv_six - 24.0)) - SHIFT_FORCE * inv, dist
+
+
+def within(dist, limit):
+    return (dist < limit) & (dist > 0.25)
+
+
+def add_pair(acc, mine, theirs, limit):
+    away, weight, dist = pair_weight(mine, theirs)
+    weight = jnp.where(within(dist, limit), weight, 0.0)
     for k in range(3):
         term = weight * away[k]
         acc[k] = term if acc[k] is None else acc[k] + term
@@ -286,9 +293,42 @@
     leaving = pltpu.make_async_copy(moved, moved_out, sem)
     leaving.start()
     row_frames(own, frames)
-    table = {kz: limits(None, mask, None, kz, 0, 1) for kz in (-2, -1, 0, 1, 2)}
-    add_pairs(frames, None, total, lambda k, x, m: own[k, x, m - 2], lambda kz, dx, g: table[kz],
-              (0, 1, 2, 3), (2, 3))
+    spots = [(k, x, yy) for k in range(3) for x in range(4) for yy in range(2)]
+    home = dict.fromkeys(spots)
+    for kz in (1, 2, 0):
+        limit = limits(None, mask, None, kz, 0, 1)
+        back = limit
+        if kz > 0:
+            same = jnp.broadcast_to(mask[0, 4:5, :], (8, ATOMS))
+            other = from_cell_below(jnp.broadcast_to(mask[0, 1:2, :], (8, ATOMS)))
+            back = jnp.where(rows8() < kz, other, same) * CUT_SQ
+        for x in range(4):
+            for yy in range(2):
+                mine = [frames[kz + 2, k, x, yy] for k in range(3)]
+                acc = [home[k, x, yy] if kz == 0 else None for k in range(3)]
+                for kx in (-2, -1, 0, 1, 2):
+                    for ky in (-1, 0, 1):
+                        if kz == 0 and (kx, ky) <= (0, 0) or not in_range(kx, ky, kz):
+                            continue
+                        if x + kx not in range(4) or yy + ky not in range(2):
+                            continue
+                        theirs = [own[k, x + kx, yy + ky] for k in range(3)]
+                        away, weight, dist = pair_weight(mine, theirs)
+                        for k in range(3):
+                            term = jnp.where(within(dist, limit), weight, 0.0) * away[k]
+                            acc[k] = term if acc[k] is None else acc[k] + term
+                            term = jnp.where(within(dist, back), weight, 0.0) * away[k]
+                            spot = k, x + kx, yy + ky
+                            home[spot] = -term if home[spot] is None else home[spot] - term
+                for k in range(3):
+                    if kz == 0:
+                        home[k, x, yy] = acc[k]
+                    else:
+                        total[kz + 2, k, x, yy] = acc[k]
+    for k, x, yy in spots:
+        total[2, k, x, yy] = home[k, x, yy]
+        total[0, k, x, yy] = jnp.zeros((8, ATOMS), F32)
+        total[1, k, x, yy] = jnp.zeros((8, ATOMS), F32)
     leaving.wait()
 
 
@@ -341,45 +381,43 @@
               lambda kz, dx, g: outer[kz + 2, g // 2], (0, 1, 2, 3), (0, 1, 4, 5))
 
 
-def row_kernel(face_a, face_b, frames, total_in, table, base, side):
+def row_kernel(s, face, frames, total_in, table, after, base, side):
     lo = low_half()
     for k in range(3):
         for n in range(2):
-            first, second = face_a[k, n], face_b[k, n]
-            for s in range(2):
-                zero, one = [(second if s == 0 else first)[yy] for yy in range(2)]
-                side[s, k, n, 0] = zero
-                side[s, k, n, 1] = one
-                side[s, k, n, 2] = swap_halves(zero)
-                side[s, k, n, 3] = swap_halves(one)
-                side[s, k, n, 4] = swap_halves(jnp.where(lo, one, zero))
-
-    for x in range(4):
+            zero, one = face[k, n, 0], face[k, n, 1]
+            side[k, n, 0] = zero
+            side[k, n, 1] = one
+            side[k, n, 2] = swap_halves(zero)
+            side[k, n, 3] = swap_halves(one)
+            side[k, n, 4] = swap_halves(jnp.where(lo, one, zero))
+
+    for x in (2 * s, 2 * s + 1):
         parts = [[{} for _ in range(3)] for _ in range(3)]
         for kz in (-2, -1, 0, 1, 2):
             mine = [[frames[kz + 2, k, x, yy] for k in range(3)] for yy in range(2)]
             inner = [jnp.where(lo, mine[1][k], mine[0][k]) for k in range(3)]
             acc = [[total_in[kz + 2, k, x, yy] for k in range(3)] for yy in range(2)]
             cross = [None] * 3
+            limit = table[kz + 2, s, 0]
             for kx in (-2, -1, 1, 2):
                 if 0 <= x + kx < 4:
                     continue
-                s, n = (0, x + kx + 2) if kx < 0 else (1, x + kx - 4)
-                limit = table[kz + 2, s, 0]
+                n = x + kx - 4 if s else x + kx + 2
                 for yy in range(2):
                     for i, ky in ((0, -yy), (1, 1 - yy), (2 + yy, 2)):
                         if in_range(kx, ky, kz):
-                            add_pair(acc[yy], mine[yy], [side[s, k, n, i] for k in range(3)], limit)
+                            add_pair(acc[yy], mine[yy], [side[k, n, i] for k in range(3)], limit)
                 if in_range(kx, 1, kz):
-                    add_pair(cross, inner, [side[s, k, n, 4] for k in range(3)], limit)
+                    add_pair(cross, inner, [side[k, n, 4] for k in range(3)], limit)
             for k in range(3):
                 parts[0][k][kz], parts[1][k][kz] = acc[0][k], acc[1][k]
                 if cross[k] is not None:
                     parts[2][k][kz] = cross[k]
         for k in range(3):
             zero, one, cross = [row_frame(parts[i][k]) for i in range(3)]
-            base[k, x, 0] = zero + jnp.where(lo, 0.0, cross)
-            base[k, x, 1] = one + jnp.where(lo, cross, 0.0)
+            base[k, x - 2 * s, 0] = zero + jnp.where(lo, 0.0, cross)
+            base[k, x - 2 * s, 1] = one + jnp.where(lo, cross, 0.0)
 
 
 def add_corners(got, frames, table, base, total, upper):
@@ -405,25 +443,24 @@
             outer_parts[k][kz] = on_outer[k]
             if on_inner[k] is not None:
                 inner_parts[k][kz], inset_parts[k][kz] = on_inner[k], on_inset[k]
-    total[...] = base[...]
     for k in range(3):
         on_outer, on_inner, on_inset = row_frame(outer_parts[k]), row_frame(inner_parts[k]), row_frame(inset_parts[k])
-        total[k, edge, 0] = base[k, edge, 0] + jnp.where(lo, on_outer, on_inner)
-        total[k, edge, 1] = base[k, edge, 1] + jnp.where(lo, on_inner, on_outer)
-        total[k, inset, 0] = base[k, inset, 0] + jnp.where(lo, on_inset, 0.0)
-        total[k, inset, 1] = base[k, inset, 1] + jnp.where(lo, 0.0, on_inset)
+        for at, zero, one in ((edge, (on_outer, on_inner), (on_inner, on_outer)),
+                              (inset, (on_inset, 0.0), (0.0, on_inset))):
+            total[k, at - 2 * side, 0] = base[k, at - 2 * side, 0] + jnp.where(lo, *zero)
+            total[k, at - 2 * side, 1] = base[k, at - 2 * side, 1] + jnp.where(lo, *one)
 
 
 def first_corner_kernel(got, frames, table, base, total):
     add_corners(got, frames, table, base, total, False)
 
 
-def finish_kernel(got, frames, table, base, half, code, vel_out, frc_out, total, new_vel, new_frc, sems):
+def finish_kernel(got, frames, table, base, lower, half, code, vel_out, frc_out, total, new_vel, new_frc, sems):
     add_corners(got, frames, table, base, total, True)
     lo = low_half()
     copies = []
     for k in range(3):
-        lattice = total[k].reshape(CELLS, ATOMS)
+        lattice = jnp.concatenate([lower[k].reshape(32, ATOMS), total[k].reshape(32, ATOMS)], axis=0)
         flipped = jnp.swapaxes(jnp.concatenate([lattice, lattice], axis=0), 0, 1)
         cells_first = jnp.where(lo[0:1], flipped[:CELLS], flipped[CELLS:])
         for g in range(8):
@@ -508,15 +545,21 @@
         [own, mask, got_a, got_b, frames, total], flops=10**8, name="column",
         scratch=[pltpu.VMEM((3, 4, 4, 8, ATOMS), F32), pltpu.VMEM((5, 2, 8, ATOMS), F32)],
     )
-    (base,) = kernel_call(
-        row_kernel, [lattice], [face_a, face_b, frames, total, table], flops=10**8, name="rows",
-        scratch=[pltpu.VMEM((2, 3, 2, 5, 8, ATOMS), F32)],
-    )
-    (base,) = kernel_call(first_corner_kernel, [lattice], [far_b, frames, table, base], flops=10**7, name="corners")
+    def rows(side, name, *args):
+        return kernel_call(
+            functools.partial(row_kernel, side), [f32(3, 2, 2, 8, ATOMS)], args, flops=10**8,
+            name=name, scratch=[pltpu.VMEM((3, 2, 5, 8, ATOMS), F32)],
+        )[0]
+
+    upper = rows(1, "upper_rows", face_a, frames, total, table, mask)
+    lower = rows(0, "lower_rows", face_b, frames, total, table, upper)
+    (lower,) = kernel_call(
+        first_corner_kernel, [f32(3, 2, 2, 8, ATOMS)], [far_b, frames, table, lower], flops=10**7, name="corners"
+    )
     new_vel, new_frc = kernel_call(
-        finish_kernel, [span, span], [far_a, frames, table, base, half, code], flops=10**8,
+        finish_kernel, [span, span], [far_a, frames, table, upper, lower, half, code], flops=10**8,
         name="finish", outs_specs=[HBM, HBM],
-        scratch=[pltpu.VMEM(lattice.shape, F32), pltpu.VMEM(span.shape, F32), pltpu.VMEM(span.shape, F32),
+        scratch=[pltpu.VMEM((3, 2, 2, 8, ATOMS), F32), pltpu.VMEM(span.shape, F32), pltpu.VMEM(span.shape, F32),
                  pltpu.SemaphoreType.DMA((6,))],
     )
     return tuple(jnp.transpose(a, (1, 0, 2)) for a in (moved, new_vel, new_frc))

time: 17.6 us -> 17.6 us (level)
  Pallas kernels: 5.94 us -> 5.65 us
  waiting for transfers between devices: 0.06 us -> 0.34 us
    pallas_call x7 -> x8, Pallas kernels: 5.94 us -> 5.65 us  [kernel_call(): pl.pallas_call(body, out_shape=outs, in_specs=[VMEM] * len(args) if specs...]
    ppermute x2, waiting for transfers between devices: 0.05 us -> 0.33 us  [pass_round(): from_lower = lax.ppermute(first, axis, up)]
  transfers between devices with their start and end apart: 6 -> 6, of which waited for: 0 -> 1; matrix products, arithmetic and copies ran while one was open for 0% -> 0% of each run, Pallas kernels for 17% -> 15%
where the time goes in v3:
time: 17.6 us; the launch traced here: 17.4 us
  starting transfers between devices  10.1 us (57%)
  Pallas kernels  5.65 us (32%)
  between operations  1.35 us (8%)
  waiting for transfers between devices  0.34 us (2%)
    pallas_call x8, Pallas kernels, kernel_call(): pl.pallas_call(body, out_shape=outs, in_specs=[VMEM] * len(args) if specs...  5.65 us
    ppermute x1, starting transfers between devices, exchange(): lax.ppermute(first, axis, pairing(count, True))  4.57 us
    ppermute x2, starting transfers between devices, pass_round(): return (lax.ppermute(second, axis, down), from_lower)  3.47 us
    ppermute x2, starting transfers between devices, pass_round(): from_lower = lax.ppermute(first, axis, up)  2.01 us
  transfers between devices with their start and end apart: 6, of which 1 were waited for; matrix products, arithmetic and copies ran while one was open for 0% of the time, Pallas kernels for 15%

profile of v3, /device:TPU:0, one launch (start us, length us, event | category | flops | bytes accessed | tf_op | source)
XLA Modules:
  0.0 17.4 jit_solution(11132098634711483560)
XLA Ops:
  1.3 1.8 %prepare.1 = (f32[3,64,128]{2,1,0:T(8,128)S(1)}, f32[3,64,128]{2,1,0:T(8,128)S(1)}, s32[64,128]{1,0:T(8,128)S(1)}, f32[3,4,2,8,128]{4,3,2,1,0:T(8,128)S(1)}, f32...) custom-call(f32[3,64,128]{2,1,0:T(8,128)} %bitcast.9, ...), custom_call_target="tpu_custom_call" | custom-call | bytes 851972 | tf_op jit(solution)/shard_map/prepare/pallas_call | solution.py:482
  3.0 4.6 %collective-permute-start = (f32[14,8,128]{2,1,0:T(8,128)S(1)}, f32[14,8,128]{2,1,0:T(8,128)S(1)}, u32[]{:S(2)}, u32[]{:S(2)}) collective-permute-start(f32[14,8,128]{2,1,0:T(8,128)S(1)} %get-tuple-element.25), channel_id=1, source_target_pairs={{0,7},{1,2},{2,1},{3,4},{4,3},{5,6},{6,5},{7,0},{8,15},{9,10},{10,... | collective-permute-start | bytes 172040 | tf_op jit(solution)/shard_map/ppermute | solution.py:502
  7.6 0.0 collective-permute-start.1
  7.6 2.4 %collective-permute-start.3 = (f32[3,2,2,8,128]{4,3,2,1,0:T(8,128)S(1)}, f32[3,2,2,8,128]{4,3,2,1,0:T(8,128)S(1)}, u32[]{:S(2)}, u32[]{:S(2)}) collective-permute-start(f32[3,2,2,8,128]{4,3,2,1,0:T(8,128)S(1)} %get-tuple-element.31), channel_id=1, source_target_pairs={{8,0},{16,8},{24,16},{0,24},{9,1},{17,9},{25,17},{1,25},{10,2},{18... | collective-permute-start | bytes 147464 | tf_op jit(solution)/shard_map/ppermute | solution.py:510
  10.1 0.0 collective-permute-start.5
  10.1 0.0 collective-permute-done.got_a
  10.1 0.0 collective-permute-done.1.got_b
  10.1 2.0 %collective-permute-start.4 = (f32[3,3,8,128]{3,2,1,0:T(8,128)S(1)}, f32[3,3,8,128]{3,2,1,0:T(8,128)S(1)}, u32[]{:S(2)}, u32[]{:S(2)}) collective-permute-start(f32[3,3,8,128]{3,2,1,0:T(8,128)S(1)} %get-tuple-element.33), channel_id=1, source_target_pairs={{0,8},{8,16},{16,24},{24,0},{1,9},{9,17},{17,25},{25,1},{2,10},{10... | collective-permute-start | bytes 110600 | tf_op jit(solution)/shard_map/ppermute | solution.py:509
  12.1 1.0 %collective-permute-start.2 = (f32[3,3,8,128]{3,2,1,0:T(8,128)S(1)}, f32[3,3,8,128]{3,2,1,0:T(8,128)S(1)}, u32[]{:S(2)}, u32[]{:S(2)}) collective-permute-start(f32[3,3,8,128]{3,2,1,0:T(8,128)S(1)} %get-tuple-element.27), channel_id=1, source_target_pairs={{8,0},{16,8},{24,16},{0,24},{9,1},{17,9},{25,17},{1,25},{10,2},{18... | collective-permute-start | bytes 110600 | tf_op jit(solution)/shard_map/ppermute | solution.py:510
  13.1 0.7 %own.1 = (f32[5,3,4,2,8,128]{5,4,3,2,1,0:T(8,128)S(1)}, f32[5,3,4,2,8,128]{5,4,3,2,1,0:T(8,128)S(1)}, f32[3,64,128]{2,1,0:T(8,128)}) custom-call(f32[3,4,2,8,128]{4,3,2,1,0:T(8,128)S(1)} %get-tuple-element.21.own, f32[2,8,128]{2,1,0:T(8,128)S(1)} %get-tuple-element.22.mask.after, f32[3,64,128]{2,1,0:T(8,128)S(1)} %get-tuple-element.23.moved), custom_call_target="tpu_custom_call" | custom-call | flops 100000000 | bytes 1286144 | tf_op jit(solution)/shard_map/own/pallas_call | solution.py:482
  13.8 1.0 %column.1 = (f32[5,3,4,2,8,128]{5,4,3,2,1,0:T(8,128)S(1)}, f32[5,2,2,8,128]{4,3,2,1,0:T(8,128)S(1)}) custom-call(f32[3,4,2,8,128]{4,3,2,1,0:T(8,128)S(1)} %get-tuple-element.21.own, f32[2,8,128]{2,1,0:T(8,128)S(1)} %get-tuple-element.22.mask.after, f32[14,8,128]{2,1,0:T(8,128)S(1)} %collective-permute-done.got_a, ...), custom_call_target="tpu_custom_call" | custom-call | flops 100000000 | bytes 1777664 | tf_op jit(solution)/shard_map/column/pallas_call | solution.py:482
  14.9 0.0 collective-permute-done.3.face
  14.9 0.4 %upper_rows.1.after.base = f32[3,2,2,8,128]{4,3,2,1,0:T(8,128)S(1)} custom-call(f32[3,2,2,8,128]{4,3,2,1,0:T(8,128)S(1)} %collective-permute-done.3.face, f32[5,3,4,2,8,128]{5,4,3,2,1,0:T(8,128)S(1)} %get-tuple-element.28.frames, f32[5,3,4,2,8,128]{5,4,3,2,1,0:T(8,128)S(1)} %get-tuple-element.32.total_in, f32[5,2,2,8,128]{4,3,2,1,0:T(8,128)S(1)} %get-tuple-element.30.table, ...), custom_call_target="tpu_custom_call" | custom-call | flops 100000000 | bytes 1171456 | tf_op jit(solution)/shard_map/upper_rows/pallas_call | solution.py:482
  15.2 0.0 collective-permute-done.5.face
  15.2 0.4 %lower_rows.1.base = f32[3,2,2,8,128]{4,3,2,1,0:T(8,128)S(1)} custom-call(f32[3,2,2,8,128]{4,3,2,1,0:T(8,128)S(1)} %collective-permute-done.5.face, f32[5,3,4,2,8,128]{5,4,3,2,1,0:T(8,128)S(1)} %get-tuple-element.28.frames, f32[5,3,4,2,8,128]{5,4,3,2,1,0:T(8,128)S(1)} %get-tuple-element.32.total_in, f32[5,2,2,8,128]{4,3,2,1,0:T(8,128)S(1)} %get-tuple-element.30.table, ...), custom_call_target="tpu_custom_call" | custom-call | flops 100000000 | bytes 1212416 | tf_op jit(solution)/shard_map/lower_rows/pallas_call | solution.py:482
  15.6 0.3 %collective-permute-done.4.got = f32[3,3,8,128]{3,2,1,0:T(8,128)S(1)} collective-permute-done((f32[3,3,8,128]{3,2,1,0:T(8,128)S(1)}, f32[3,3,8,128]{3,2,1,0:T(8,128)S(1)}, u32[]{:S(2)}, u32[]{:S(2)}) %collective-permute-start.4) | collective-permute-done | bytes 36896 | tf_op jit(solution)/shard_map/ppermute | solution.py:509
  15.9 0.2 %corners.1.lower = f32[3,2,2,8,128]{4,3,2,1,0:T(8,128)S(1)} custom-call(f32[3,3,8,128]{3,2,1,0:T(8,128)S(1)} %collective-permute-done.4.got, f32[5,3,4,2,8,128]{5,4,3,2,1,0:T(8,128)S(1)} %get-tuple-element.28.frames, f32[5,2,2,8,128]{4,3,2,1,0:T(8,128)S(1)} %get-tuple-element.30.table, f32[3,2,2,8,128]{4,3,2,1,0:T(8,128)S(1)} %lower_rows.1.base), custom_call_target="tpu_custom_call" | custom-call | flops 10000000 | bytes 708608 | tf_op jit(solution)/shard_map/corners/pallas_call | solution.py:482
  16.1 0.0 collective-permute-done.2.got
  16.1 1.2 %finish.1 = (f32[3,64,128]{2,1,0:T(8,128)}, f32[3,64,128]{2,1,0:T(8,128)}) custom-call(f32[3,3,8,128]{3,2,1,0:T(8,128)S(1)} %collective-permute-done.2.got, f32[5,3,4,2,8,128]{5,4,3,2,1,0:T(8,128)S(1)} %get-tuple-element.28.frames, f32[5,2,2,8,128]{4,3,2,1,0:T(8,128)S(1)} %get-tuple-element.30.table, f32[3,2,2,8,128]{4,3,2,1,0:T(8,128)S(1)} %upper_rows.1.after.base, ...), custom_call_target="tpu_custom_call" | custom-call | flops 100000000 | bytes 1036288 | tf_op jit(solution)/shard_map/finish/pallas_call | solution.py:482
  (1 shorter events, 0.0 us)
Async XLA Ops:
  3.0 7.0 %collective-permute-start = (f32[14,8,128]{2,1,0:T(8,128)S(1)}, f32[14,8,128]{2,1,0:T(8,128)S(1)}, u32[]{:S(2)}, u32[]{:S(2)}) collective-permute-start(f32[14,8,128]{2,1,0:T(8,128)S(1)} %get-tuple-element.25), channel_id=1, source_target_pairs={{0,7},{1,2},{2,1},{3,4},{4,3},{5,6},{6,5},{7,0},{8,15},{9,10},{10,... | collective-permute-start | bytes 172040 | tf_op jit(solution)/shard_map/ppermute | solution.py:502
  7.6 2.5 %collective-permute-start.1 = (f32[14,8,128]{2,1,0:T(8,128)S(1)}, f32[14,8,128]{2,1,0:T(8,128)S(1)}, u32[]{:S(2)}, u32[]{:S(2)}) collective-permute-start(f32[14,8,128]{2,1,0:T(8,128)S(1)} %get-tuple-element.26), channel_id=1, source_target_pairs={{0,1},{1,0},{2,3},{3,2},{4,5},{5,4},{6,7},{7,6},{8,9},{9,8},{10,11... | collective-permute-start | bytes 172040 | tf_op jit(solution)/shard_map/ppermute | solution.py:502
  7.6 7.2 %collective-permute-start.3 = (f32[3,2,2,8,128]{4,3,2,1,0:T(8,128)S(1)}, f32[3,2,2,8,128]{4,3,2,1,0:T(8,128)S(1)}, u32[]{:S(2)}, u32[]{:S(2)}) collective-permute-start(f32[3,2,2,8,128]{4,3,2,1,0:T(8,128)S(1)} %get-tuple-element.31), channel_id=1, source_target_pairs={{8,0},{16,8},{24,16},{0,24},{9,1},{17,9},{25,17},{1,25},{10,2},{18... | collective-permute-start | bytes 147464 | tf_op jit(solution)/shard_map/ppermute | solution.py:510
  10.1 5.2 %collective-permute-start.5 = (f32[3,2,2,8,128]{4,3,2,1,0:T(8,128)S(1)}, f32[3,2,2,8,128]{4,3,2,1,0:T(8,128)S(1)}, u32[]{:S(2)}, u32[]{:S(2)}) collective-permute-start(f32[3,2,2,8,128]{4,3,2,1,0:T(8,128)S(1)} %get-tuple-element.34), channel_id=1, source_target_pairs={{0,8},{8,16},{16,24},{24,0},{1,9},{9,17},{17,25},{25,1},{2,10},{10... | collective-permute-start | bytes 147464 | tf_op jit(solution)/shard_map/ppermute | solution.py:509
  10.1 5.8 %collective-permute-start.4 = (f32[3,3,8,128]{3,2,1,0:T(8,128)S(1)}, f32[3,3,8,128]{3,2,1,0:T(8,128)S(1)}, u32[]{:S(2)}, u32[]{:S(2)}) collective-permute-start(f32[3,3,8,128]{3,2,1,0:T(8,128)S(1)} %get-tuple-element.33), channel_id=1, source_target_pairs={{0,8},{8,16},{16,24},{24,0},{1,9},{9,17},{17,25},{25,1},{2,10},{10... | collective-permute-start | bytes 110600 | tf_op jit(solution)/shard_map/ppermute | solution.py:509
  12.1 4.0 %collective-permute-start.2 = (f32[3,3,8,128]{3,2,1,0:T(8,128)S(1)}, f32[3,3,8,128]{3,2,1,0:T(8,128)S(1)}, u32[]{:S(2)}, u32[]{:S(2)}) collective-permute-start(f32[3,3,8,128]{3,2,1,0:T(8,128)S(1)} %get-tuple-element.27), channel_id=1, source_target_pairs={{8,0},{16,8},{24,16},{0,24},{9,1},{17,9},{25,17},{1,25},{10,2},{18... | collective-permute-start | bytes 110600 | tf_op jit(solution)/shard_map/ppermute | solution.py:510
